TPU v7x, 32 devices: a whole 2x2x4 slice. The times are simulated.
32 devices in a mesh: dp: 8 (over y, x, core), mp: 4 (over z).
Axes of the slice: x: 2, y: 2, z: 4, core: 2. Of those that a mesh axis runs over, the one named last changes fastest.
Arguments:
- stream: float32 [768, 16384], P('mp', 'dp'), may hold values from -17 to 17
- segment_ids: int32 [8, 2048], P('dp'), may hold values from 0 to 3, as said below
- cotangent: float32 [768, 16384], P('mp', 'dp'), may hold values from -6 to 6
- ln1_gain: float32 [768], P('mp'), may hold values from 0.25 to 1.75
- qkv_weight: bfloat16 [3, 768, 768], P(None, 'mp'), may hold values from -0.21875 to 0.21875
- qv_bias: float32 [2, 768], P(None, 'mp'), may hold values from -3 to 3
- out_weight: bfloat16 [768, 768], P('mp'), may hold values from -1.75 to 1.75
- out_bias: float32 [768], replicated, may hold values from -3 to 3
- ln2_gain: float32 [768], P('mp'), may hold values from 0.25 to 1.75
- up_weight: bfloat16 [768, 3072], P(None, 'mp'), may hold values from -0.21875 to 0.21875
- up_bias: float32 [3072], P('mp'), may hold values from -3 to 3
- down_weight: bfloat16 [3072, 768], P('mp'), may hold values from -0.109375 to 0.109375
- down_bias: float32 [768], replicated, may hold values from -3 to 3
Outputs:
- mixed: float32 [768, 16384], P('mp', 'dp')
- stream_grad: float32 [768, 16384], P('mp', 'dp')
- ln1_grad: float32 [768], P('mp')
- qkv_grad: float32 [3, 768, 768], P(None, 'mp')
- qv_bias_grad: float32 [2, 768], P(None, 'mp')
- out_grad: float32 [768, 768], P('mp')
- out_bias_grad: float32 [768], replicated
- ln2_grad: float32 [768], P('mp')
- up_grad: float32 [768, 3072], P(None, 'mp')
- up_bias_grad: float32 [3072], P('mp')
- down_grad: float32 [3072, 768], P('mp')
- down_bias_grad: float32 [768], replicated
Inputs may be any that keep to these rules, and one draw needn't show every extreme that they name: `segment_ids`: half of the dp rows, which ones drawn from the seed, hold one sequence of 16384 // 8 tokens (all ids 0); the others hold 4 sequences of 512 tokens each, numbered in order.
All inputs are finite; a program needn't handle non-finite values.
Results may differ from a plain program's by a relative error of at most 0.012.
Values may be sent and summed in bfloat16 or wider, within the bound.
A program may use at most 192 MiB of HBM per device.

v0:
```python
from functools import partial

import jax
import jax.numpy as jnp
from jax import lax
from jax.sharding import PartitionSpec as P

HD = 64
QB = 512


EPS = 1e-05
NEG = -1e30


def norm_forward(values_in, gain, last_mask, stream_width):
    row_sum, square_sum = lax.psum(
        (jnp.sum(values_in, axis=0), jnp.sum(values_in * values_in, axis=0)), "mp"
    )
    inverse = lax.rsqrt((square_sum + row_sum * row_sum) / stream_width + EPS)
    recovered = jnp.where(last_mask, -row_sum[None, :], values_in)
    local_rows = (recovered * inverse[None, :] * gain[:, None]).astype(jnp.bfloat16)
    whole = lax.all_gather(local_rows, "mp", axis=0, tiled=True)
    return (whole, row_sum, inverse)


def norm_backward(
    grad_normed, values_in, gain, row_sum, inverse, keep_mask, last_mask, stream_width
):
    recovered = jnp.where(last_mask, -row_sum[None, :], values_in)
    scaled = grad_normed * gain[:, None]
    gain_grad = jnp.sum(grad_normed * recovered * inverse[None, :], axis=1)
    dot_local = jnp.sum(scaled * recovered, axis=0)
    tail_local = jnp.sum(jnp.where(last_mask, scaled, 0.0), axis=0)
    total, tail = lax.psum((dot_local, tail_local), "mp")
    cubed = inverse * inverse * inverse
    grad_in = (
        inverse[None, :] * (scaled - tail[None, :])
        - (total * cubed)[None, :] * (values_in + row_sum[None, :]) / stream_width
    )
    return (jnp.where(keep_mask, grad_in, 0.0), gain_grad)


def branch_out(inputs, weight, bias, offset, columns):
    bias_centred = bias - jnp.mean(bias)
    partial_rows = jnp.einsum("tc,cd->dt", inputs, weight, preferred_element_type=jnp.float32)
    centred = partial_rows - jnp.mean(partial_rows, axis=0, keepdims=True)
    summed = lax.psum_scatter(centred, "mp", scatter_dimension=0, tiled=True)
    return summed + lax.dynamic_slice_in_dim(bias_centred, offset, columns)[:, None]


def branch_grad(grad_next, keep_mask):
    grad_local = jnp.where(keep_mask, grad_next, 0.0).astype(jnp.bfloat16)
    full_grad = lax.all_gather(grad_local, "mp", axis=0, tiled=True).astype(jnp.float32)
    return (full_grad - jnp.mean(full_grad, axis=0, keepdims=True)).astype(jnp.bfloat16)


def input_grad(inputs, weight, pattern):
    partial_rows = jnp.einsum(pattern, inputs, weight, preferred_element_type=jnp.float32)
    return lax.psum_scatter(partial_rows, "mp", scatter_dimension=0, tiled=True)


def block_scores(query_rows, key_part, segments, positions, start_row, end_row, scale):
    raw = (
        jnp.einsum("qhe,khe->hqk", query_rows, key_part, preferred_element_type=jnp.float32) * scale
    )
    allowed = (segments[start_row:end_row, None] == segments[None, :end_row]) & (
        positions[None, :end_row] <= positions[start_row:end_row, None]
    )
    return jnp.where(allowed[None], raw, NEG)


def local(
    stream,
    segment_ids,
    cotangent,
    ln1_gain,
    qkv_weight,
    qv_bias,
    out_weight,
    out_bias,
    ln2_gain,
    up_weight,
    up_bias,
    down_weight,
    down_bias,
):
    columns, token_count = stream.shape
    stream_width = columns * lax.axis_size("mp")
    offset = lax.axis_index("mp") * columns
    column_ids = offset + lax.iota(jnp.int32, columns)
    keep_mask = (column_ids != stream_width - 1)[:, None]
    last_mask = (column_ids == stream_width - 1)[:, None]
    segments = segment_ids[0]
    positions = lax.iota(jnp.int32, token_count)
    heads_here = columns // HD
    scale = HD ** (-0.5)
    blocks_count = token_count // QB
    masked_in = jnp.where(keep_mask, stream, 0.0)
    normed_one, row_sum_one, inverse_one = norm_forward(
        masked_in, ln1_gain, last_mask, stream_width
    )
    joined = jnp.einsum("dt,kcd->tkc", normed_one, qkv_weight, preferred_element_type=jnp.float32)
    queries = (
        (joined[:, 0] + qv_bias[0][None, :])
        .astype(jnp.bfloat16)
        .reshape(token_count, heads_here, HD)
    )
    keys_in = joined[:, 1].astype(jnp.bfloat16).reshape(token_count, heads_here, HD)
    values_in = (
        (joined[:, 2] + qv_bias[1][None, :])
        .astype(jnp.bfloat16)
        .reshape(token_count, heads_here, HD)
    )
    context_parts = []
    lse_parts = []
    for block_number in range(blocks_count):
        start_row = block_number * QB
        end_row = start_row + QB
        scores = block_scores(
            queries[start_row:end_row],
            keys_in[:end_row],
            segments,
            positions,
            start_row,
            end_row,
            scale,
        )
        row_max = jnp.max(scores, axis=-1, keepdims=True)
        expo = jnp.exp(scores - row_max)
        total = jnp.sum(expo, axis=-1, keepdims=True)
        probs = expo / total
        lse_parts.append(row_max + jnp.log(total))
        context_parts.append(
            jnp.einsum(
                "hqk,khe->qhe",
                probs.astype(jnp.bfloat16),
                values_in[:end_row],
                preferred_element_type=jnp.float32,
            )
        )
    context = (
        jnp.concatenate(context_parts, axis=0).reshape(token_count, columns).astype(jnp.bfloat16)
    )
    middle = masked_in + jnp.where(
        keep_mask, branch_out(context, out_weight, out_bias, offset, columns), 0.0
    )
    normed_two, row_sum_two, inverse_two = norm_forward(middle, ln2_gain, last_mask, stream_width)
    pre_act = (
        jnp.einsum("dt,df->tf", normed_two, up_weight, preferred_element_type=jnp.float32)
        + up_bias[None, :]
    )
    activated, gelu_back = jax.vjp(partial(jax.nn.gelu, approximate=True), pre_act)
    hidden = activated.astype(jnp.bfloat16)
    mixed = middle + jnp.where(
        keep_mask, branch_out(hidden, down_weight, down_bias, offset, columns), 0.0
    )
    grad_mlp_y = branch_grad(cotangent, keep_mask)
    down_bias_grad = jnp.sum(grad_mlp_y, axis=1, dtype=jnp.float32)
    down_grad = jnp.einsum("tf,dt->fd", hidden, grad_mlp_y, preferred_element_type=jnp.float32)
    grad_hidden = jnp.einsum(
        "dt,fd->tf", grad_mlp_y, down_weight, preferred_element_type=jnp.float32
    )
    grad_pre = gelu_back(grad_hidden)[0].astype(jnp.bfloat16)
    up_bias_grad = jnp.sum(grad_pre, axis=0, dtype=jnp.float32)
    up_grad = jnp.einsum("dt,tf->df", normed_two, grad_pre, preferred_element_type=jnp.float32)
    grad_normed_two = input_grad(grad_pre, up_weight, "tf,df->dt")
    grad_middle_norm, ln2_grad = norm_backward(
        grad_normed_two,
        middle,
        ln2_gain,
        row_sum_two,
        inverse_two,
        keep_mask,
        last_mask,
        stream_width,
    )
    grad_middle = cotangent + grad_middle_norm
    grad_attn_y = branch_grad(grad_middle, keep_mask)
    out_bias_grad = jnp.sum(grad_attn_y, axis=1, dtype=jnp.float32)
    out_grad = jnp.einsum("tc,dt->cd", context, grad_attn_y, preferred_element_type=jnp.float32)
    grad_context = jnp.einsum(
        "dt,cd->tc", grad_attn_y, out_weight, preferred_element_type=jnp.float32
    )
    grad_context = grad_context.astype(jnp.bfloat16).reshape(token_count, heads_here, HD)
    grad_query_parts = []
    grad_keys = jnp.zeros((token_count, heads_here, HD), jnp.float32)
    grad_values = jnp.zeros((token_count, heads_here, HD), jnp.float32)
    for block_number in range(blocks_count):
        start_row = block_number * QB
        end_row = start_row + QB
        query_rows = queries[start_row:end_row]
        grad_rows = grad_context[start_row:end_row]
        scores = block_scores(
            query_rows, keys_in[:end_row], segments, positions, start_row, end_row, scale
        )
        probs = jnp.exp(scores - lse_parts[block_number])
        grad_probs = jnp.einsum(
            "qhe,khe->hqk", grad_rows, values_in[:end_row], preferred_element_type=jnp.float32
        )
        weighted = jnp.sum(probs * grad_probs, axis=-1, keepdims=True)
        grad_scores = (probs * (grad_probs - weighted)).astype(jnp.bfloat16)
        grad_query_parts.append(
            jnp.einsum(
                "hqk,khe->qhe", grad_scores, keys_in[:end_row], preferred_element_type=jnp.float32
            )
            * scale
        )
        key_term = (
            jnp.einsum("hqk,qhe->khe", grad_scores, query_rows, preferred_element_type=jnp.float32)
            * scale
        )
        value_term = jnp.einsum(
            "hqk,qhe->khe",
            probs.astype(jnp.bfloat16),
            grad_rows,
            preferred_element_type=jnp.float32,
        )
        padding = ((0, token_count - end_row), (0, 0), (0, 0))
        grad_keys = grad_keys + jnp.pad(key_term, padding)
        grad_values = grad_values + jnp.pad(value_term, padding)
    grad_queries = jnp.concatenate(grad_query_parts, axis=0)
    grad_joined = jnp.stack(
        [
            grad_queries.reshape(token_count, columns),
            grad_keys.reshape(token_count, columns),
            grad_values.reshape(token_count, columns),
        ],
        axis=1,
    ).astype(jnp.bfloat16)
    qv_bias_grad = jnp.stack(
        [
            jnp.sum(grad_joined[:, 0], axis=0, dtype=jnp.float32),
            jnp.sum(grad_joined[:, 2], axis=0, dtype=jnp.float32),
        ],
        axis=0,
    )
    qkv_grad = jnp.einsum(
        "dt,tkc->kcd", normed_one, grad_joined, preferred_element_type=jnp.float32
    )
    grad_normed_one = input_grad(grad_joined, qkv_weight, "tkc,kcd->dt")
    grad_in_norm, ln1_grad = norm_backward(
        grad_normed_one,
        masked_in,
        ln1_gain,
        row_sum_one,
        inverse_one,
        keep_mask,
        last_mask,
        stream_width,
    )
    stream_grad = jnp.where(keep_mask, grad_middle + grad_in_norm, 0.0)
    (
        ln1_grad,
        qkv_grad,
        qv_bias_grad,
        out_grad,
        out_bias_grad,
        ln2_grad,
        up_grad,
        up_bias_grad,
        down_grad,
        down_bias_grad,
    ) = lax.psum(
        (
            ln1_grad,
            qkv_grad,
            qv_bias_grad,
            out_grad,
            out_bias_grad,
            ln2_grad,
            up_grad,
            up_bias_grad,
            down_grad,
            down_bias_grad,
        ),
        "dp",
    )
    return (
        mixed,
        stream_grad,
        ln1_grad,
        qkv_grad,
        qv_bias_grad,
        out_grad,
        out_bias_grad,
        ln2_grad,
        up_grad,
        up_bias_grad,
        down_grad,
        down_bias_grad,
    )


def solution(mesh):
    return jax.shard_map(
        local,
        mesh=mesh,
        in_specs=(
            P("mp", "dp"),
            P("dp", None),
            P("mp", "dp"),
            P("mp"),
            P(None, "mp", None),
            P(None, "mp"),
            P("mp", None),
            P(),
            P("mp"),
            P(None, "mp"),
            P("mp"),
            P("mp", None),
            P(),
        ),
        out_specs=(
            P("mp", "dp"),
            P("mp", "dp"),
            P("mp"),
            P(None, "mp", None),
            P(None, "mp"),
            P("mp", None),
            P(),
            P("mp"),
            P(None, "mp"),
            P("mp"),
            P("mp", None),
            P(),
        ),
        check_vma=False,
    )
```

profile of v0, /device:TPU:1, one launch (start us, length us, event | category | flops | bytes accessed | tf_op | source)
XLA Modules:
  0.0 1009.5 jit_solution(2414178505125860568)
XLA Ops:
  9.2 16.2 %all-reduce.11 = (f32[2048]{0:T(1024)S(1)}, f32[2048]{0:T(1024)S(1)}) all-reduce(f32[2048]{0:T(1024)S(1)} %get-tuple-element.19, f32[2048]{0:T(1024)S(1)} %get-tuple-element.18), channel_id=1, replica_groups=mesh['dp'=8,'mp'=4] {'mp'}, use_global_device_ids=true, to_apply=%region_3.4 | all-reduce | flops 4096 | bytes 32768 | tf_op jit(solution)/shard_map/psum | solution.py:17
  35.0 59.3 %all-gather.5.cloned.1.call-done = bf16[768,2048]{1,0:T(8,128)(2,1)} async-done(((bf16[192,2048]{1,0:T(8,128)(2,1)}), bf16[768,2048]{1,0:T(8,128)(2,1)}) %all-gather.5.cloned.1.call-update) | async-done | bytes 3145744 | tf_op jit(solution)/shard_map/all_gather | solution.py:23
  135.0 107.1 %reduce-scatter.5.cloned.1.call-done = f32[192,2048]{1,0:T(8,128)} async-done(((f32[768,2048]{1,0:T(8,128)}), f32[192,2048]{1,0:T(8,128)}) %reduce-scatter.5.cloned.1.call-update) | async-done | bytes 1572880 | tf_op jit(solution)/shard_map/reduce_scatter | solution.py:48
  245.7 15.0 %all-reduce.10 = (f32[2048]{0:T(1024)}, f32[2048]{0:T(1024)}) all-reduce(f32[2048]{0:T(1024)} %get-tuple-element.21, f32[2048]{0:T(1024)S(1)} %get-tuple-element.20), channel_id=1, replica_groups=mesh['dp'=8,'mp'=4] {'mp'}, use_global_device_ids=true, to_apply=%region_18.19 | all-reduce | flops 4096 | bytes 32768 | tf_op jit(solution)/shard_map/psum | solution.py:17
  266.5 63.7 %all-gather.7.cloned.1.call-done = bf16[768,2048]{1,0:T(8,128)(2,1)} async-done(((bf16[192,2048]{1,0:T(8,128)(2,1)}), bf16[768,2048]{1,0:T(8,128)(2,1)}) %all-gather.7.cloned.1.call-update) | async-done | bytes 3145744 | tf_op jit(solution)/shard_map/all_gather | solution.py:23
  330.2 5.0 fusion.111
  342.3 52.2 %all-gather.9.cloned.1.call-done = bf16[768,2048]{1,0:T(8,128)(2,1)} async-done(((bf16[192,2048]{1,0:T(8,128)(2,1)}), bf16[768,2048]{1,0:T(8,128)(2,1)}) %all-gather.9.cloned.1.call-update) | async-done | bytes 3145744 | tf_op jit(solution)/shard_map/all_gather | solution.py:54
  397.3 9.5 convert_reduce_fusion.3
  408.4 4.6 convolution_bitcast_fusion.1
  415.0 91.1 %reduce-scatter.7.cloned.1.call-done = f32[192,2048]{1,0:T(8,128)} async-done(((f32[768,2048]{1,0:T(8,128)}), f32[192,2048]{1,0:T(8,128)}) %reduce-scatter.7.cloned.1.call-update) | async-done | bytes 1572880 | tf_op jit(solution)/shard_map/reduce_scatter | solution.py:48
  506.1 113.5 %reduce-scatter.9.cloned.1.call-done = f32[192,2048]{1,0:T(8,128)} async-done(((f32[768,2048]{1,0:T(8,128)}), f32[192,2048]{1,0:T(8,128)}) %reduce-scatter.9.cloned.1.call-update) | async-done | bytes 1572880 | tf_op jit(solution)/shard_map/reduce_scatter | solution.py:60
  619.6 4.6 multiply_reduce_fusion.4
  624.1 14.4 %all-reduce.9 = (f32[2048]{0:T(1024)S(1)}, f32[2048]{0:T(1024)S(1)}) all-reduce(f32[2048]{0:T(1024)S(1)} %get-tuple-element.15, f32[2048]{0:T(1024)S(1)} %get-tuple-element.16), channel_id=1, replica_groups=mesh['dp'=8,'mp'=4] {'mp'}, use_global_device_ids=true, to_apply=%region_27.28 | all-reduce | flops 4096 | bytes 32768 | tf_op jit(solution)/shard_map/psum | solution.py:35
  642.8 65.4 %all-gather.11.cloned.1.call-done = bf16[768,2048]{1,0:T(8,128)(2,1)} async-done(((bf16[192,2048]{1,0:T(8,128)(2,1)}), bf16[768,2048]{1,0:T(8,128)(2,1)}) %all-gather.11.cloned.1.call-update) | async-done | bytes 3145744 | tf_op jit(solution)/shard_map/all_gather | solution.py:54
  730.5 4.7 multiply_reduce_fusion.1
  735.2 6.2 multiply_convert_fusion.1
  754.3 5.0 fusion.85
  763.0 4.6 convolution_bitcast_fusion
  767.9 7.0 fusion.112
  774.9 8.9 fusion.53
  793.1 84.2 %reduce-scatter.11.cloned.1.call-done = f32[192,2048]{1,0:T(8,128)} async-done(((f32[768,2048]{1,0:T(8,128)}), f32[192,2048]{1,0:T(8,128)}) %reduce-scatter.11.cloned.1.call-update) | async-done | bytes 1572880 | tf_op jit(solution)/shard_map/reduce_scatter | solution.py:60
  879.6 21.9 %all-reduce.6 = (f32[192]{0:T(256)}, f32[2,192]{1,0:T(2,128)}, f32[768]{0:T(1024)}, f32[192]{0:T(256)}, f32[768]{0:T(1024)}, /*index=5*/f32[768]{0:T(1024)}) all-reduce(f32[192]{0:T(256)S(1)} %get-tuple-element.12, f32[2,192]{1,0:T(2,128)S(1)} %pad_maximum_fusion.5, ...), channel_id=1, replica_groups=mesh['dp'=8,'mp'=4] {'dp'}, use_global_device_ids=true, to_apply=%region_39.40 | all-reduce | flops 3072 | bytes 24576 | tf_op jit(solution)/shard_map/psum | solution.py:264
  901.5 14.5 %all-reduce.8 = (f32[2048]{0:T(1024)S(1)}, f32[2048]{0:T(1024)S(1)}) all-reduce(f32[2048]{0:T(1024)S(1)} %get-tuple-element.13, f32[2048]{0:T(1024)S(1)} %get-tuple-element.17), channel_id=1, replica_groups=mesh['dp'=8,'mp'=4] {'mp'}, use_global_device_ids=true, to_apply=%region_37.38 | all-reduce | flops 4096 | bytes 32768 | tf_op jit(solution)/shard_map/psum | solution.py:35
  919.8 76.4 %all-reduce.14.cloned.1.call-done = (f32[3,192,768]{2,1,0:T(8,128)}, f32[192,768]{1,0:T(8,128)}, f32[768,768]{1,0:T(8,128)}, f32[768,768]{1,0:T(8,128)}) async-done(((f32[3,192,768]{2,1,0:T(8,128)}, f32[192,768]{1,0:T(8,128)}, f32[768,768]{1,0:T(8,128)}, f32[768,768]{1,0:T(8,128)}), (f32[3,192,768]{2,1,0:T(8,128)}, f32[192,768]{1,0:T(8,128)}, f32[768,768]{1,0:T(8,128)}, ...) | async-done | bytes 7077904 | tf_op jit(solution)/shard_map/psum | solution.py:264
  (367 shorter events, 137.9 us)
Async XLA Ops:
  7.2 328.0 %copy-start = (bf16[768,768]{1,0:T(8,128)(2,1)S(1)}, bf16[768,768]{1,0:T(8,128)(2,1)}, u32[]{:S(2)}) copy-start(bf16[768,768]{1,0:T(8,128)(2,1)} %param.24) | copy-start | bytes 3538948
  7.2 87.1 %all-gather.5.cloned.1.call-start = ((), (), s32[]{:S(2)}) async-start(), calls=%async_computation.4 | async-start | bytes 3932160 | tf_op jit(solution)/shard_map/all_gather | solution.py:23
  28.7 213.3 %reduce-scatter.5.cloned.1.call-start = ((), (), s32[]{:S(2)}) async-start(), calls=%async_computation.5 | async-start | bytes 7864320 | tf_op jit(solution)/shard_map/reduce_scatter | solution.py:48
  28.9 93.1 %copy-start.72 = (f32[3,64]{1,0:T(4,128)}, f32[3,64]{1,0:T(4,128)S(1)}, u32[]{:S(2)}) copy-start(f32[3,64]{1,0:T(4,128)S(1)} %add.231) | copy-start | bytes 2308
  132.4 109.7 %copy-start.7 = (f32[192,2048]{1,0:T(8,128)S(1)}, f32[192,2048]{1,0:T(8,128)}, u32[]{:S(2)}) copy-start(f32[192,2048]{1,0:T(8,128)} %param.13) | copy-start | bytes 4718596
  132.4 197.8 %all-gather.7.cloned.1.call-start = ((), (), s32[]{:S(2)}) async-start(), calls=%async_computation.6 | async-start | bytes 3932160 | tf_op jit(solution)/shard_map/all_gather | solution.py:23
  264.7 129.7 %all-gather.9.cloned.1.call-start = ((), (), s32[]{:S(2)}) async-start(), calls=%async_computation.8 | async-start | bytes 3932160 | tf_op jit(solution)/shard_map/all_gather | solution.py:54
  266.5 239.6 %reduce-scatter.7.cloned.1.call-start = ((), (), s32[]{:S(2)}) async-start(), calls=%async_computation.7 | async-start | bytes 7864320 | tf_op jit(solution)/shard_map/reduce_scatter | solution.py:48
  342.0 277.5 %reduce-scatter.9.cloned.1.call-start = ((), (), s32[]{:S(2)}) async-start(), calls=%async_computation.9 | async-start | bytes 7864320 | tf_op jit(solution)/shard_map/reduce_scatter | solution.py:60
  413.0 206.6 %copy-start.9 = (f32[192,2048]{1,0:T(8,128)S(1)}, f32[192,2048]{1,0:T(8,128)}, u32[]{:S(2)}) copy-start(f32[192,2048]{1,0:T(8,128)} %get-tuple-element.42) | copy-start | bytes 4718596
  413.0 206.6 %copy-start.69 = (f32[2048]{0:T(1024)S(1)}, f32[2048]{0:T(1024)}, u32[]{:S(2)}) copy-start(f32[2048]{0:T(1024)} %copy-done.68) | copy-start | bytes 24580
  413.0 206.6 %copy-start.90 = (pred[192]{0:T(512)(128)(4,1)S(1)}, pred[192]{0:T(512)(128)(4,1)}, u32[]{:S(2)}) copy-start(pred[192]{0:T(512)(128)(4,1)} %copy-done.89) | copy-start | bytes 580
  413.0 206.6 %copy-start.95 = (f32[192]{0:T(256)S(1)}, f32[192]{0:T(256)}, u32[]{:S(2)}) copy-start(f32[192]{0:T(256)} %param.21) | copy-start | bytes 2308
  413.0 206.6 %copy-start.97 = (pred[192]{0:T(512)(128)(4,1)S(1)}, pred[192]{0:T(512)(128)(4,1)}, u32[]{:S(2)}) copy-start(pred[192]{0:T(512)(128)(4,1)} %copy-done.96) | copy-start | bytes 580
  413.0 295.1 %all-gather.11.cloned.1.call-start = ((), (), s32[]{:S(2)}) async-start(), calls=%async_computation.10 | async-start | bytes 3932160 | tf_op jit(solution)/shard_map/all_gather | solution.py:54
  415.0 223.5 %copy-start.88 = (f32[2048]{0:T(1024)S(1)}, f32[2048]{0:T(1024)}, u32[]{:S(2)}) copy-start(f32[2048]{0:T(1024)} %get-tuple-element.37) | copy-start | bytes 24580
  642.6 234.7 %reduce-scatter.11.cloned.1.call-start = ((), (), s32[]{:S(2)}) async-start(), calls=%async_computation.11 | async-start | bytes 7864320 | tf_op jit(solution)/shard_map/reduce_scatter | solution.py:60
  767.7 228.5 %all-reduce.14.cloned.1.call-start = ((), (), s32[]{:S(2)}) async-start(), calls=%async_computation.12 | async-start | bytes 14155776 | tf_op jit(solution)/shard_map/psum | solution.py:264
  791.9 85.4 %copy-start.8 = (f32[192,2048]{1,0:T(8,128)S(1)}, f32[192,2048]{1,0:T(8,128)}, u32[]{:S(2)}) copy-start(f32[192,2048]{1,0:T(8,128)} %param.13) | copy-start | bytes 4718596
  792.0 85.4 %copy-start.60 = (f32[2048]{0:T(1024)S(1)}, f32[2048]{0:T(1024)}, u32[]{:S(2)}) copy-start(f32[2048]{0:T(1024)} %copy-done.59) | copy-start | bytes 24580
  792.0 85.4 %copy-start.67 = (f32[2048]{0:T(1024)S(1)}, f32[2048]{0:T(1024)}, u32[]{:S(2)}) copy-start(f32[2048]{0:T(1024)} %copy-done.66) | copy-start | bytes 24580
  792.4 87.2 %copy-start.99 = (f32[768]{0:T(1024)S(1)}, f32[768]{0:T(1024)}, u32[]{:S(2)}) copy-start(f32[768]{0:T(1024)} %get-tuple-element.85) | copy-start | bytes 9220
  792.4 87.2 %copy-start.100 = (f32[192]{0:T(256)S(1)}, f32[192]{0:T(256)}, u32[]{:S(2)}) copy-start(f32[192]{0:T(256)} %get-tuple-element.14) | copy-start | bytes 2308
  792.4 123.5 %copy-start.87 = (f32[2048]{0:T(1024)S(1)}, f32[2048]{0:T(1024)}, u32[]{:S(2)}) copy-start(f32[2048]{0:T(1024)} %copy-done.86) | copy-start | bytes 24580
  (106 other events, 1083.6 us)
Sparse Core Ops, SparseCore 0:
  28.8 65.4 all-gather.4
  132.5 109.4 reduce-scatter.4
  264.8 65.3 all-gather.6
  332.2 62.1 all-gather.8
  396.6 109.4 reduce-scatter.6
  508.2 111.2 reduce-scatter.8
  642.7 65.3 all-gather.10
  767.8 109.4 reduce-scatter.10
  882.2 114.0 all-reduce.13
where the time goes:
time: 1020 us; the launch traced here: 1010 us
  waiting for transfers between devices  713 us (70%)
  matrix products  107 us (10%)
  blocking collectives  82 us (8%)
  other arithmetic  69.1 us (7%)
  local copies, waits for them, and re-layouts  20.6 us (2%)
  between operations  16.8 us (2%)
    reduce_scatter x2, waiting for transfers between devices, branch_out(): summed = lax.psum_scatter(centred, 'mp', scatter_dimension=0, tiled=True)  198 us
    reduce_scatter x2, waiting for transfers between devices, input_grad(): return lax.psum_scatter(partial_rows, 'mp', scatter_dimension=0, tiled=True)  198 us
    all_gather x2, waiting for transfers between devices, norm_forward(): whole = lax.all_gather(local_rows, 'mp', axis=0, tiled=True)  123 us
    all_gather x2, waiting for transfers between devices, branch_grad(): lax.all_gather(grad_local, 'mp', axis=0, tiled=True).astype(jnp.float32)  118 us
    psum x1, waiting for transfers between devices, local(): lax.psum((ln1_grad, qkv_grad, qv_bias_grad, out_grad, out_bias_grad, ln2_...  76.4 us
    psum x2, blocking collectives, norm_forward(): lax.psum((jnp.sum(values_in, axis=0), jnp.sum(values_in * values_in, axis...  31.3 us
    psum x2, blocking collectives, norm_backward(): total, tail = lax.psum((dot_local, tail_local), 'mp')  28.8 us
    psum x1, blocking collectives, local(): lax.psum((ln1_grad, qkv_grad, qv_bias_grad, out_grad, out_bias_grad, ln2_...  21.9 us
  transfers between devices with their start and end apart: 9, of which 9 were waited for; matrix products, arithmetic and copies ran while one was open for 7% of the time, Pallas kernels for 0%

commit v1 on v0

v1 whole, which is shorter than its diff:
```python
import functools

import jax
import jax.numpy as jnp
from jax import lax
from jax.experimental import pallas as pl
from jax.experimental.pallas import tpu as pltpu
from jax.sharding import Mesh, PartitionSpec as P

HD = 64
QB = 512
GROUP = 4
EPS = 1e-05
NEG = -1e30
MESH = pl.DeviceIdType.MESH
BF = jnp.bfloat16
F32 = jnp.float32
ALL = ("blk", "do", "di", "mp")
ROWS = ("blk", "do", "di")


def places():
    return lax.axis_index("do"), lax.axis_index("di"), lax.axis_index("mp")


def holder(row, quarter):
    return lax.rem(quarter, 2), 2 * row + quarter // 2


def dev(do, di, mp):
    return (lax.axis_index("blk"), do, di, mp)


def flip(index, bit):
    return index + bit * (1 - 2 * lax.rem(index // bit, 2))


def remote(source, target, send, recv, device):
    return pltpu.make_async_remote_copy(
        source, target, send, recv, device_id=device, device_id_type=MESH
    )


def greet(others):
    barrier = pltpu.get_barrier_semaphore()
    for other in others:
        pl.semaphore_signal(barrier, inc=1, device_id=other, device_id_type=MESH)
    pl.semaphore_wait(barrier, len(others))


def neighbours(do, di, mp):
    column = [
        dev(do, lax.rem(di + a, 2), lax.rem(mp + b, GROUP))
        for a in range(2)
        for b in range(GROUP)
        if a or b
    ]
    return column + [dev(flip(do, 1), di, mp), dev(flip(do, 2), di, mp)]


def send_block(source, target, send, recv, place, target_place, do):
    (di, mp), (tdi, tmp) = place, target_place
    other = jnp.logical_or(tdi != di, tmp != mp)

    @pl.when(other)
    def _():
        remote(source, target, send, recv, dev(do, tdi, tmp)).start()

    @pl.when(jnp.logical_not(other))
    def _():
        pltpu.make_async_copy(source, target, recv).start()


def sent_block(source, target, send, recv, place, target_place, do):
    (di, mp), (tdi, tmp) = place, target_place
    other = jnp.logical_or(tdi != di, tmp != mp)

    @pl.when(other)
    def _():
        remote(source, target, send, recv, dev(do, tdi, tmp)).wait_send()


def piece_of(ref, do, di):
    rows, lanes = ref.shape[0] // GROUP, ref.shape[1] // 2
    return ref.at[
        pl.ds(pl.multiple_of(do * rows, rows), rows), pl.ds(pl.multiple_of(di * lanes, lanes), lanes)
    ]


def pieces_of(weight):
    return weight.reshape(GROUP, 2, weight.shape[0] // (2 * GROUP), weight.shape[1])


def dot_nt(left, right):
    return lax.dot_general(left, right, (((1,), (1,)), ((), ())), preferred_element_type=F32)


def dot_tn(left, right):
    return lax.dot_general(left, right, (((0,), (0,)), ((), ())), preferred_element_type=F32)


def add_pairs(count, target, first, second):
    def step(i, carry):
        ref = target(i)
        ref[...] = (first(i)[...].astype(F32) + second(i)[...].astype(F32)).astype(ref.dtype)
        return carry

    lax.fori_loop(0, count, step, 0)


def backward_kernel(
    gctx_ref, delta_ref, x_ref, gn2_ref, heads_ref, rest_ref, qkv_ref, lse_ref, normed_ref,
    smalls_ref, headw_ref, segs_ref, stat_ref, sums_ref, dup_ref, oup_ref, ddown_ref, odown_ref, dout_ref,
    m_ref, s_ref, qkvg_ref, small_out, up_out, down_out, out_out,
    gall, k_tok, v_tok, causal, acc_k, acc_v, gj, acc_w, acc_b, gain_wide, acc_gain,
    part, near, total, far_buf, s_blocks,
    core_out, mine_up, mine_down, mine_out,
    one_up, one_down, one_out, two_up, two_down, two_out, z_up, z_down, z_out,
    fin_up, fin_down, fin_out, gq, q_one, q_two, q_z, q_fin, small_a, small_b, small_z,
    own_sem, b_send, b_recv, r_send, r_recv, send, recv,
):
    do, di, mp = places()
    width, tokens = x_ref.shape
    columns = heads_ref.shape[1]
    heads = columns // HD
    row, quarter, half = mp // 2, own_quarter(di, mp), lax.rem(mp, 2)
    place = (di, mp)
    sibling, across = dev(do, 1 - di, mp), dev(do, di, flip(mp, 1))
    posted, pending = [], []

    def prepare(source, target, device):
        n = len(posted)
        copy = remote(source, target, send.at[n], recv.at[n], device)
        posted.append(copy)
        pending.append(copy)
        return copy

    def post(source, target, device):
        copy = prepare(source, target, device)
        copy.start()
        return copy

    def finish(copy):
        copy.wait()
        pending[:] = [other for other in pending if other is not copy]

    def arrived(copies):
        for copy in copies:
            copy.wait_recv()

    def column(bit):
        return dev(flip(do, bit), di, mp)

    grads = (
        (dup_ref, mine_up, oup_ref, one_up, two_up, z_up, fin_up, up_out, 1, 2),
        (ddown_ref, mine_down, odown_ref, one_down, two_down, z_down, fin_down, down_out, 2, 1),
        (dout_ref, mine_out, core_out, one_out, two_out, z_out, fin_out, out_out, 1, 2),
    )
    own = []
    for i, g in enumerate(grads[:2]):
        for n, piece in enumerate((do, flip(do, g[9]))):
            own.append(pltpu.make_async_copy(g[0].at[piece], g[1].at[piece], own_sem.at[4 + 2 * i + n]))
        own.append(pltpu.make_async_copy(g[2], g[3], own_sem.at[8 + i]))
    own.append(pltpu.make_async_copy(dout_ref.at[:, di], mine_out, own_sem.at[2]))
    for copy in own:
        copy.start()
    greet(neighbours(do, di, mp))

    swaps = []
    for k in range(GROUP):
        swaps.append(
            (
                gctx_ref.at[k], gall.at[quarter], b_send.at[k], b_recv.at[quarter], place,
                holder(row, k), do,
            )
        )
        send_block(*swaps[k])
    stage_core = [post(dout_ref.at[:, 1 - di], core_out, sibling)]

    def turn(step, carry):
        h, kb = step // GROUP, lax.rem(step, GROUP)
        rows = pl.ds(pl.multiple_of(columns + h * HD, HD), HD)
        k_tok[h, kb] = qkv_ref[kb, rows].T
        rows = pl.ds(pl.multiple_of(2 * columns + h * HD, HD), HD)
        v_tok[h, kb] = qkv_ref[kb, rows].T
        return carry

    lax.fori_loop(0, heads * GROUP, turn, 0)
    causal[...] = jnp.where(
        lax.broadcasted_iota(jnp.int32, causal.shape, 0)
        <= lax.broadcasted_iota(jnp.int32, causal.shape, 1),
        0.0, NEG,
    )
    for j in range(GROUP):
        turned = smalls_ref[j].T[:columns, 0:1]
        gain_wide[j * columns : (j + 1) * columns] = jnp.broadcast_to(turned, (columns, 128))
    acc_b[...] = jnp.zeros_like(acc_b)
    acc_w[...] = jnp.zeros_like(acc_w)
    segments = segs_ref[row]
    head_weight = headw_ref[...].reshape(3 * columns, width)
    def back_block(block):
        seg_q = segments[:, block * tokens : (block + 1) * tokens]
        masks = [
            jnp.where(segments[:, kb * tokens : kb * tokens + 1] == seg_q, 0.0, NEG)
            for kb in range(block)
        ]

        def one_head(h, carry):
            rows = pl.ds(pl.multiple_of(h * HD, HD), HD)
            k_rows = pl.ds(pl.multiple_of(columns + h * HD, HD), HD)
            query = qkv_ref[block, rows] * HD ** (-0.5)
            grad = gall[block, rows]
            mixed = heads_ref[block, rows].astype(F32) + rest_ref[block, rows].astype(F32)
            weighted = jnp.sum(grad.astype(F32) * mixed, axis=0, keepdims=True)
            lse = lse_ref[h, block, 0:1]
            grad_query = jnp.zeros((HD, tokens), F32)
            for kb in range(block + 1):
                raw = jnp.dot(k_tok[h, kb], query, preferred_element_type=F32)
                raw = raw + (causal[...] if kb == block else masks[kb])
                probs = jnp.exp(raw - lse)
                grad_probs = jnp.dot(v_tok[h, kb], grad, preferred_element_type=F32)
                grad_scores = (probs * (grad_probs - weighted)).astype(BF)
                grad_query += jnp.dot(qkv_ref[kb, k_rows], grad_scores, preferred_element_type=F32)
                key_term = dot_nt(query, grad_scores)
                value_term = dot_nt(grad, probs.astype(BF))
                if block == GROUP - 1:
                    acc_k[kb, rows] = key_term
                    acc_v[kb, rows] = value_term
                else:
                    acc_k[kb, rows] += key_term
                    acc_v[kb, rows] += value_term
            gj[rows] = (grad_query * HD ** (-0.5)).astype(BF)
            return carry

        lax.fori_loop(0, heads, one_head, 0)
        gj[columns : 2 * columns] = acc_k[block].astype(BF)
        gj[2 * columns :] = acc_v[block].astype(BF)
        part[block] = dot_tn(head_weight, gj[...])

    def near_args(i):
        return part.at[i], near.at[i // 2], r_send.at[i], r_recv.at[i], sibling

    def far_args(i):
        return total, far_buf, r_send.at[GROUP + i], r_recv.at[GROUP + i], across

    def to_sibling(i):
        @pl.when(di != i % 2)
        def _():
            remote(*near_args(i)).start()

    def across_row(i):
        @pl.when(di == i % 2)
        def _():
            remote(*near_args(i)).wait_recv()
            at = lambda k: pl.ds(pl.multiple_of(k * columns, columns), columns)
            add_pairs(
                GROUP,
                lambda k: near.at[i // 2, at(k)],
                lambda k: near.at[i // 2, at(k)],
                lambda k: part.at[i, at(k)],
            )

            @pl.when(half != i // 2)
            def _():
                total[...] = near[i // 2].astype(BF)
                remote(*far_args(i)).start()

    def weight_terms(block):
        acc_w[...] += dot_nt(gj[...], normed_ref[block])
        terms = gj[...].astype(F32)
        for k in range(tokens // 128):
            acc_b[: 3 * columns] += terms[:, k * 128 : (k + 1) * 128]

    def stage_one():
        arrived(stage_core)
        own[-1].wait()
        g = grads[2]
        add_pairs(
            GROUP * GROUP,
            lambda n: mine_out.at[n // GROUP, lax.rem(n, GROUP)],
            lambda n: mine_out.at[n // GROUP, lax.rem(n, GROUP)],
            lambda n: core_out.at[n // GROUP, lax.rem(n, GROUP)],
        )
        pieces = (flip(do, g[8]), flip(flip(do, g[8]), g[9]))
        return [post(mine_out.at[p], one_out.at[n], column(g[8])) for n, p in enumerate(pieces)]

    def stage_two(chosen):
        later = []
        for g in chosen:
            mine, one, first, second = g[1], g[3], g[8], g[9]
            for n, piece in ((1, flip(do, second)), (0, do)):
                add_pairs(
                    mine.shape[1], lambda k: mine.at[piece, k], lambda k: mine.at[piece, k],
                    lambda k: one.at[n, k],
                )
                if n == 1:
                    later.append(post(mine.at[piece], g[4], column(second)))
        return later

    def stage_three(copies, chosen):
        arrived(copies)
        later = []
        for g in chosen:
            mine, two, z_buf = g[1], g[4], g[5]
            add_pairs(
                mine.shape[1], lambda k: mine.at[do, k], lambda k: mine.at[do, k],
                lambda k: two.at[k],
            )
            for r in range(1, GROUP):
                later.append(
                    post(mine.at[do, r], z_buf.at[r - 1], dev(do, di, lax.rem(mp + r, GROUP)))
                )
        return later

    def stage_four(copies):
        arrived(copies)
        later = []
        for i, g in enumerate(grads):
            mine, z_buf, fin = g[1], g[5], g[6]
            fin[...] = (
                mine[do, 0].astype(F32) + z_buf[0].astype(F32)
                + z_buf[1].astype(F32) + z_buf[2].astype(F32)
            )
            pltpu.make_async_copy(fin, g[7].at[do, di], own_sem.at[i]).start()
            later.append(post(fin, g[7].at[do, di], column(g[8])))
        return later

    def stage_five(copies):
        arrived(copies)
        later = []
        for i, g in enumerate(grads):
            pltpu.make_async_copy(g[6], g[7].at[do, di], own_sem.at[i]).wait()
            for piece in (do, flip(do, g[8])):
                later.append(post(g[7].at[piece, di], g[7].at[piece, di], column(g[9])))
        return later

    def stage_six(copies):
        arrived(copies)
        return [post(g[7].at[:, di], g[7].at[:, di], sibling) for g in grads]

    for copy in own[:-1]:
        copy.wait()
    copies = stage_two(grads[:2])
    for k in range(GROUP):
        pltpu.make_async_copy(gctx_ref.at[k], gall.at[k], b_recv.at[k]).wait()
    for k in range(GROUP):
        swaps.append(
            (
                delta_ref.at[k], m_ref.at[quarter], b_send.at[GROUP + k],
                b_recv.at[GROUP + quarter], place, (row, k), do,
            )
        )
        send_block(*swaps[GROUP + k])
    back_block(3)
    to_sibling(3)
    weight_terms(3)
    out_copies = stage_one()
    copies = stage_three(copies, grads[:2])
    back_block(2)
    to_sibling(2)
    across_row(3)
    weight_terms(2)
    arrived(out_copies)
    out_copies = stage_two(grads[2:])
    back_block(1)
    to_sibling(1)
    across_row(2)
    weight_terms(1)
    copies += stage_three(out_copies, grads[2:])
    back_block(0)
    to_sibling(0)
    across_row(1)
    weight_terms(0)
    across_row(0)

    wide = width // 2
    sides = (pl.ds(0, wide), pl.ds(wide, wide))
    bits = ((1, 2), (2, 1))
    gq[...] = acc_w[...].astype(BF).reshape(gq.shape)
    q_copies = []
    for side, (first, second) in enumerate(bits):
        for n, piece in enumerate((flip(do, first), flip(flip(do, first), second))):
            q_copies.append(post(gq.at[piece, :, sides[side]], q_one.at[side, n], column(first)))
    copies = stage_four(copies)

    @pl.when(half == 0)
    def _():
        for i in (0, 1):
            @pl.when(di == i)
            def _():
                remote(*far_args(i)).wait_recv()

    @pl.when(half == 1)
    def _():
        for i in (2, 3):
            @pl.when(di == i - 2)
            def _():
                remote(*far_args(i)).wait_recv()

    acc_gain[...] = jnp.zeros_like(acc_gain)

    def norm_step(lane, carry):
        lanes = pl.ds(pl.multiple_of(lane * 128, 128), 128)
        values = x_ref[:, lanes]
        grad = near[half, :, lanes] + far_buf[:, lanes].astype(F32)
        row_sum, inverse = stat_ref[0:1, lanes], stat_ref[1:2, lanes]
        final = lax.broadcasted_iota(jnp.int32, (width, 128), 0) == width - 1
        recovered = jnp.where(final, -row_sum, values)
        scaled = grad * gain_wide[...]
        acc_gain[...] += grad * recovered * inverse
        dot_sum = jnp.sum(scaled * recovered, axis=0, keepdims=True)
        tail = scaled[width - 1 :]
        factor = dot_sum * (inverse * inverse * inverse) / width
        grad_in = inverse * (scaled - tail) - factor * (values + row_sum)
        grad_in = jnp.where(final, 0.0, grad_in) + gn2_ref[:, lanes].astype(F32)
        for j in range(GROUP):
            s_blocks[j, :, lanes] = grad_in[j * columns : (j + 1) * columns].astype(BF)
        return carry

    lax.fori_loop(0, tokens // 128, norm_step, 0)
    for k in range(GROUP):
        swaps.append(
            (
                s_blocks.at[k], s_ref.at[quarter], b_send.at[2 * GROUP + k],
                b_recv.at[2 * GROUP + quarter], place, (row, k), do,
            )
        )
        send_block(*swaps[2 * GROUP + k])

    small_a[...] = jnp.zeros_like(small_a)
    small_a[0] = jnp.sum(acc_gain[...].T, axis=0, keepdims=True)
    bias_row = jnp.sum(acc_b[...].T, axis=0, keepdims=True)
    for r in range(3):
        small_a[1 + r] = sums_ref[r]
    for r in range(GROUP):
        small_a[4 + lax.rem(mp + r, GROUP)] = sums_ref[3 + r]
    small_a[8 + 2 * quarter, :, :columns] = bias_row[:, :columns]
    small_a[9 + 2 * quarter, :, :columns] = bias_row[:, 2 * columns : 3 * columns]
    small_one = post(small_a, small_b.at[0], sibling)

    arrived(q_copies)
    q_copies = []
    for side, (first, second) in enumerate(bits):
        for n, piece in ((1, flip(do, second)), (0, do)):
            gq[piece, :, sides[side]] = (
                gq[piece, :, sides[side]].astype(F32) + q_one[side, n].astype(F32)
            ).astype(BF)
            if n == 1:
                q_copies.append(post(gq.at[piece, :, sides[side]], q_two.at[side], column(second)))
    finish(small_one)
    small_a[...] += small_b[0]
    small_one = post(small_a, small_b.at[1], column(1))
    copies = stage_five(copies)
    arrived(q_copies)
    z_args = []
    for side in range(2):
        gq[do, :, sides[side]] = (
            gq[do, :, sides[side]].astype(F32) + q_two[side].astype(F32)
        ).astype(BF)
        z_args.append(
            (
                gq.at[do, :, sides[side]], q_z.at[row], b_send.at[3 * GROUP + side],
                b_recv.at[3 * GROUP + row], place, (side, quarter), do,
            )
        )
        send_block(*z_args[side])
    finish(small_one)
    small_a[...] += small_b[1]
    small_one = post(small_a, small_b.at[2], column(2))

    for r in range(2):
        pltpu.make_async_copy(q_z.at[r], q_z.at[r], b_recv.at[3 * GROUP + r]).wait()
    q_fin[...] = q_z[0].astype(F32) + q_z[1].astype(F32)

    def q_ref(piece, core):
        return qkvg_ref.at[piece, core]

    q_own = pltpu.make_async_copy(q_fin, q_ref(do, di), own_sem.at[3])
    q_own.start()
    q_copies = [post(q_fin, q_ref(do, di), column(bit)) for bit in (1, 2)]
    finish(small_one)
    small_z[mp] = small_a[...] + small_b[2]
    small_copies = [
        post(small_z.at[mp], small_z.at[mp], dev(do, di, lax.rem(mp + r, GROUP)))
        for r in range(1, GROUP)
    ]
    copies = stage_six(copies)
    arrived(q_copies)

    q_last = prepare(q_ref(do, di), q_ref(do, di), sibling)
    n = len(posted) - 1

    @pl.when(di == 0)
    def _():
        piece = q_ref(flip(do, 1), di)
        remote(piece, piece, send.at[n], recv.at[n], column(2)).start()

    @pl.when(di == 1)
    def _():
        piece = q_ref(flip(do, 2), di)
        remote(piece, piece, send.at[n], recv.at[n], column(1)).start()

    q_own.wait()
    q_last.wait_recv()
    q_copies = [post(qkvg_ref.at[:, di], qkvg_ref.at[:, di], sibling)]
    arrived(small_copies)
    small_out[...] = small_z[0] + small_z[1] + small_z[2] + small_z[3]
    arrived(q_copies)

    for k in range(GROUP):
        pltpu.make_async_copy(delta_ref.at[k], m_ref.at[k], b_recv.at[GROUP + k]).wait()
        pltpu.make_async_copy(s_blocks.at[k], s_ref.at[k], b_recv.at[2 * GROUP + k]).wait()
    for args in swaps + z_args:
        sent_block(*args)
    for i in range(GROUP):
        @pl.when(di != i % 2)
        def _():
            remote(*near_args(i)).wait_send()

        @pl.when(jnp.logical_and(di == i % 2, half != i // 2))
        def _():
            remote(*far_args(i)).wait_send()

    arrived(copies)
    for copy in pending:
        copy.wait_send()


def backward_part(values):
    (
        grad_context, delta, x_mine, grad_norm, heads_out, _, qkv, lse, normed, smalls,
        head_weight, segs, _, sums, up_grad, _, down_grad, _, out_grad,
    ) = values
    columns, tokens = heads_out.shape[1:]
    width = x_mine.shape[0]
    heads = columns // HD
    shape = jax.ShapeDtypeStruct
    vmem, anywhere = pl.BlockSpec(memory_space=pltpu.VMEM), pl.BlockSpec(memory_space=pl.ANY)
    dma = pltpu.SemaphoreType.DMA
    slabs = (GROUP, columns, tokens)
    pieces = head_weight.shape[1]
    weight_grads = (up_grad, down_grad, out_grad)
    rows = [w.shape[-2:] for w in weight_grads]
    halves = [(GROUP, GROUP) + r for r in rows]
    buffers = (
        halves[2:]
        + halves
        + [(2, GROUP) + r for r in rows]
        + [(GROUP,) + r for r in rows]
        + [(GROUP - 1,) + r for r in rows]
    )
    return pl.pallas_call(
        backward_kernel,
        out_shape=[
            shape(slabs, BF),
            shape(slabs, BF),
            shape((GROUP, 2, pieces, width // 2), F32),
            shape((16, 1, width), F32),
        ]
        + [shape((GROUP, 2) + r, F32) for r in rows],
        in_specs=[vmem] * 14 + [anywhere] * 5,
        out_specs=[vmem] * 4 + [anywhere] * 3,
        scratch_shapes=[
            pltpu.VMEM(slabs, BF),
            pltpu.VMEM((heads, GROUP, tokens, HD), BF),
            pltpu.VMEM((heads, GROUP, tokens, HD), BF),
            pltpu.VMEM((tokens, tokens), F32),
            pltpu.VMEM(slabs, F32),
            pltpu.VMEM(slabs, F32),
            pltpu.VMEM((3 * columns, tokens), BF),
            pltpu.VMEM((3 * columns, width), F32),
            pltpu.VMEM((640, 128), F32),
            pltpu.VMEM((width, 128), F32),
            pltpu.VMEM((width, 128), F32),
            pltpu.VMEM((GROUP, width, tokens), F32),
            pltpu.VMEM((2, width, tokens), F32),
            pltpu.VMEM((width, tokens), BF),
            pltpu.VMEM((width, tokens), BF),
            pltpu.VMEM(slabs, BF),
        ]
        + [pltpu.VMEM(b, BF) for b in buffers]
        + [pltpu.VMEM(r, F32) for r in rows]
        + [
            pltpu.VMEM((GROUP, pieces, width), BF),
            pltpu.VMEM((2, 2, pieces, width // 2), BF),
            pltpu.VMEM((2, pieces, width // 2), BF),
            pltpu.VMEM((2, pieces, width // 2), BF),
            pltpu.VMEM((pieces, width // 2), F32),
            pltpu.VMEM((16, 1, width), F32),
            pltpu.VMEM((3, 16, 1, width), F32),
            pltpu.VMEM((GROUP, 16, 1, width), F32),
            dma((10,)),
            dma((14,)),
            dma((14,)),
            dma((2 * GROUP,)),
            dma((2 * GROUP,)),
            dma((56,)),
            dma((56,)),
        ],
        compiler_params=pltpu.CompilerParams(
            collective_id=7, has_side_effects=True, vmem_limit_bytes=60 * 2**20
        ),
    )(*values)


def own_quarter(di, mp):
    return 2 * lax.rem(mp, 2) + di


def lane_chunks(count, step):
    lax.fori_loop(
        0, count, lambda i, c: (step(pl.ds(pl.multiple_of(i * 128, 128), 128)), c)[1], 0
    )


def xor(index, mask):
    for bit in (1, 2):
        if mask & bit:
            index = flip(index, bit)
    return index


def first_kernel(
    stream_ref, cot_ref, seg_ref, small_ref, bias_ref, qkvw_ref, up_own, down_own, out_own,
    mine_ref, heads_ref, rest_ref, qkv_ref, lse_ref, normed_ref, smalls_ref, headw_ref, segs_ref,
    stat_ref, delta_ref, gctx_ref, gnorm_ref, sums_ref, mine_up, one_up, mine_down, one_down, dout_ref,
    up_all, down_all, out_all,
    grad_ref, context_ref, k_tokens, big, causal, wide_gain, back_gain, n2t, gyt,
    stats, x_more, g_more,
    w_up, w_down, w_out, d_up, d_down, n2, gy, pre, ghid, hidden, gpre, mlp, gn2, acc_gain,
    core_up, core_down,
    own_sem, in_sem, w_sem, x_send, x_recv, g_send, g_recv, c_send, c_recv, s_send, s_recv,
    st_send, st_recv, r_send, r_recv, h_send, h_recv, a_send, a_recv, t_send, t_recv, k_send, k_recv, o_send, o_recv,
):
    do, di, mp = places()
    width, tokens = normed_ref.shape[1], normed_ref.shape[2]
    columns = stream_ref.shape[0]
    heads_here = columns // HD
    lanes_count = tokens // 128
    row, quarter = mp // 2, own_quarter(di, mp)
    place = (di, mp)
    sibling, across = dev(do, 1 - di, mp), dev(do, di, flip(mp, 1))
    far = 2 * (1 - lax.rem(mp, 2)) + di
    weights = ((up_own, up_all), (down_own, down_all), (out_own, out_all))
    final = lax.broadcasted_iota(jnp.int32, (width, 128), 0) == width - 1

    def column(bit):
        return dev(flip(do, bit), di, mp)

    loads = []
    for i, ref in enumerate((stream_ref, cot_ref)):
        for k in range(GROUP):
            loads.append(
                pltpu.make_async_copy(
                    ref.at[:, pl.ds(k * tokens, tokens)],
                    big.at[pl.ds(i * width + k * columns, columns)],
                    own_sem.at[2 + GROUP * i + k],
                )
            )
    own = [
        pltpu.make_async_copy(small_ref, smalls_ref.at[mp], own_sem.at[0]),
        pltpu.make_async_copy(seg_ref, segs_ref.at[di], own_sem.at[1]),
    ]
    for copy in loads + own:
        copy.start()
    greet(neighbours(do, di, mp))
    is_last = jnp.logical_and(
        mp == GROUP - 1, lax.broadcasted_iota(jnp.int32, (columns, tokens), 0) == columns - 1
    )

    def target_of(k):
        return lax.rem(k, 2), 2 * di + k // 2

    def rows_at(j):
        return pl.ds(pl.multiple_of(j * columns, 64), columns)

    def others():
        return [dev(do, di, lax.rem(mp + r, GROUP)) for r in range(1, GROUP)]

    x_rest = [n2t.at[pl.ds(k * columns, columns)] for k in range(GROUP)]
    g_rest = [gnorm_ref.at[pl.ds(k * columns, columns)] for k in range(GROUP)]

    for k in range(GROUP):
        loads[k].wait()
        rows_k = pl.ds(k * columns, columns)
        part = jnp.where(is_last, 0.0, big[rows_k])
        big[rows_k] = part
        stats[mp, k, 0:1] = jnp.sum(part, axis=0, keepdims=True)
        stats[mp, k, 1:2] = jnp.sum(part * part, axis=0, keepdims=True)
    sums_over = [
        remote(stats.at[mp], stats.at[mp], st_send.at[r], st_recv.at[GROUP - r - 1], other)
        for r, other in zip(range(GROUP - 1), others())
    ]
    for copy in sums_over:
        copy.start()
    smalls = []
    for r in range(1, GROUP):
        target = dev(do, di, lax.rem(mp + r, GROUP))
        smalls.append(
            remote(small_ref, smalls_ref.at[mp], s_send.at[r], s_recv.at[GROUP - r], target)
        )
    smalls.append(remote(seg_ref, segs_ref.at[di], s_send.at[0], s_recv.at[0], sibling))
    for copy in smalls:
        copy.start()
    own_turned = small_ref[...].T
    own_gain = own_turned[:columns, 0:1]
    for copy in sums_over:
        copy.wait_recv()
    x_args, stat_args, x_rest_args = [], [], []
    for k in range(GROUP):
        row_sum = stats[0, k, 0:1] + stats[1, k, 0:1] + stats[2, k, 0:1] + stats[3, k, 0:1]
        squares = stats[0, k, 1:2] + stats[1, k, 1:2] + stats[2, k, 1:2] + stats[3, k, 1:2]
        mean = (squares + row_sum * row_sum) / width + EPS
        inverse = lax.rsqrt(mean)
        stats[GROUP, k, 0:1] = row_sum
        stats[GROUP, k, 1:2] = inverse
        stats[GROUP, k, 2:3] = 1.0 / inverse
        values = big[k * columns : (k + 1) * columns]
        recovered = jnp.where(is_last, -row_sum, values)
        normed = (recovered * inverse * own_gain).astype(BF)
        delta_ref[k] = normed
        x_args.append(
            (
                delta_ref.at[k], normed_ref.at[k, rows_at(mp)], x_send.at[k], x_recv.at[mp],
                place, target_of(k), do,
            )
        )
        send_block(*x_args[k])
        near = (normed.astype(F32) * (1.0 / own_gain)) * stats[GROUP, k, 2:3]
        x_rest[k][...] = jnp.where(is_last, 0.0, values - near).astype(BF)
        stat_args.append(
            (stats.at[GROUP, k], stat_ref, r_send.at[k], r_recv.at[0], place, target_of(k), do)
        )
        x_rest_args.append(
            (
                x_rest[k], x_more.at[mp], r_send.at[GROUP + k], r_recv.at[1 + mp],
                place, target_of(k), do,
            )
        )

    @pl.when(mp == 0)
    def _():
        for args in stat_args:
            send_block(*args)

    head_target = (lax.rem(mp, 2), mp // 2 + 2 * di)
    head_args = (
        qkvw_ref.at[do], headw_ref.at[do], h_send.at[0], h_recv.at[0], place, head_target, do,
    )
    send_block(*head_args)

    gathers = []
    for k in range(GROUP):
        j = xor(mp, k)
        part = normed_ref.at[quarter, rows_at(j)]
        pltpu.make_async_copy(part, part, x_recv.at[j]).wait()
        for lane, other in enumerate((across, sibling)):
            copy = remote(part, part, g_send.at[lane, k], g_recv.at[lane, k], other)
            copy.start()
            gathers.append(copy)

    def over_mp(i, r):
        ref, all_ref = weights[i]
        return remote(
            ref.at[do, di] if i < 2 else piece_of(ref, do, di), all_ref.at[do, di, r],
            a_send.at[i, r], a_recv.at[i, r], dev(do, di, lax.rem(mp + GROUP - r, GROUP)),
        )

    for r in range(1, GROUP):
        over_mp(2, r).start()
    for i in range(2):
        over_mp(i, 1).start()

    orders = ((1, 2), (2, 1))

    def hop(i, r, stage):
        all_ref = weights[i][1]
        first, second = orders[i]
        if stage == 3:
            ref = all_ref.at[:, di, r]
            return [remote(ref, ref, t_send.at[i, r, 3], t_recv.at[i, r, 3], sibling)]
        pieces = (do,) if stage == 1 else (do, flip(do, first))
        bit = first if stage == 1 else second
        copies = []
        for n, piece in enumerate(pieces):
            ref = all_ref.at[piece, di, r]
            at = stage - 1 + n
            copies.append(remote(ref, ref, t_send.at[i, r, at], t_recv.at[i, r, at], column(bit)))
        return copies

    def out_hop(stage):
        if stage == 3:
            ref = out_all.at[:, di, pl.ds(1, GROUP - 1)]
            return [remote(ref, ref, t_send.at[0, 0, 3], t_recv.at[0, 0, 3], sibling)]
        pieces = (do,) if stage == 1 else (do, flip(do, 1))
        copies = []
        for n, piece in enumerate(pieces):
            ref = out_all.at[piece, di, pl.ds(1, GROUP - 1)]
            at = stage - 1 + n
            copies.append(
                remote(ref, ref, t_send.at[0, 0, at], t_recv.at[0, 0, at], column(stage))
            )
        return copies

    def start(copies):
        for copy in copies:
            copy.start()

    def arrived(copies):
        for copy in copies:
            copy.wait_recv()

    def both(r, stage):
        return hop(0, r, stage) + hop(1, r, stage)

    pltpu.make_async_copy(qkvw_ref.at[do], headw_ref.at[do], h_recv.at[0]).wait()
    cut = 80
    part_a, part_b = pl.ds(0, cut), pl.ds(cut, headw_ref.shape[1] - cut)
    heads = []

    def head_copy(piece, part, bit):
        ref = headw_ref.at[piece, part]
        n = len(heads) + 1
        copy = remote(ref, ref, h_send.at[n], h_recv.at[n], column(bit))
        copy.start()
        heads.append(copy)

    head_copy(do, part_a, 1)
    head_copy(do, part_b, 2)

    arrived(smalls)
    for copy in own:
        copy.wait()
    for j in range(GROUP):
        turned = smalls_ref[j].T
        at = slice(j * columns, (j + 1) * columns)
        back_gain[at] = jnp.broadcast_to(1.0 / turned[:columns, 0:1], (columns, 128))
        wide_gain[at] = jnp.broadcast_to(turned[columns : 2 * columns, 0:1], (columns, 128))
    biases = smalls_ref[quarter].T
    query_bias = biases[2 * columns : 3 * columns, 0:1]
    value_bias = biases[3 * columns :, 0:1]
    causal[...] = jnp.where(
        lax.broadcasted_iota(jnp.int32, causal.shape, 0)
        <= lax.broadcasted_iota(jnp.int32, causal.shape, 1),
        0.0, NEG,
    )
    for k in range(GROUP):
        loads[GROUP + k].wait()
        part = jnp.where(is_last, 0.0, big[width + k * columns : width + (k + 1) * columns])
        gctx_ref[k] = part.astype(BF)
        g_rest[k][...] = (part - gctx_ref[k].astype(F32)).astype(BF)
    arrived(heads[:2])
    head_copy(do, part_a, 2)
    head_copy(flip(do, 1), part_a, 2)
    head_copy(do, part_b, 1)
    head_copy(flip(do, 2), part_b, 1)
    for k in range(GROUP):
        gathers[2 * k].wait_recv()
        part = normed_ref.at[far, rows_at(xor(mp, 1 ^ k))]
        copy = remote(part, part, g_send.at[2, k], g_recv.at[2, k], sibling)
        copy.start()
        gathers.append(copy)
    for k in range(GROUP):
        gathers[2 * k + 1].wait_recv()
        gathers[2 * GROUP + k].wait_recv()
    arrived(heads[2:])
    cot_args = [
        (gctx_ref.at[k], grad_ref.at[mp], c_send.at[k], c_recv.at[mp], place, target_of(k), do)
        for k in range(GROUP)
    ]
    for args in cot_args:
        send_block(*args)
    g_rest_args = [
        (
            g_rest[k], g_more.at[mp], r_send.at[2 * GROUP + k], r_recv.at[1 + GROUP + mp],
            place, target_of(k), do,
        )
        for k in range(GROUP)
    ]
    head_weight = headw_ref[...].reshape(3 * columns, width)

    def project(block, carry):
        joined = jnp.dot(head_weight, normed_ref[block], preferred_element_type=F32)
        qkv_ref[block, :columns] = (joined[:columns] + query_bias).astype(BF)
        keys = joined[columns : 2 * columns].astype(BF)
        qkv_ref[block, columns : 2 * columns] = keys
        qkv_ref[block, 2 * columns :] = (joined[2 * columns :] + value_bias).astype(BF)
        for h in range(heads_here):
            k_tokens[h, block] = keys[h * HD : (h + 1) * HD].T
        return carry

    lax.fori_loop(0, GROUP, project, 0)
    segments = segs_ref[row]

    def attend(block):
        seg_q = segments[:, block * tokens : (block + 1) * tokens]
        masks = [
            jnp.where(segments[:, kb * tokens : kb * tokens + 1] == seg_q, 0.0, NEG)
            for kb in range(block)
        ]

        def one_head(h, carry):
            rows = pl.ds(pl.multiple_of(h * HD, HD), HD)
            v_rows = pl.ds(pl.multiple_of(2 * columns + h * HD, HD), HD)
            query = qkv_ref[block, rows] * HD ** (-0.5)
            top = None
            for kb in range(block + 1):
                raw = jnp.dot(k_tokens[h, kb], query, preferred_element_type=F32)
                raw = raw + (causal[...] if kb == block else masks[kb])
                big[kb * tokens : (kb + 1) * tokens] = raw
                high = jnp.max(raw, axis=0, keepdims=True)
                top = high if top is None else jnp.maximum(top, high)
            total = jnp.zeros((1, tokens), F32)
            for kb in range(block + 1):
                expo = jnp.exp(big[kb * tokens : (kb + 1) * tokens] - top)
                big[kb * tokens : (kb + 1) * tokens] = expo
                total += jnp.sum(expo, axis=0, keepdims=True)
            portion = 1.0 / total
            mixed = jnp.zeros((HD, tokens), F32)
            for kb in range(block + 1):
                probs = (big[kb * tokens : (kb + 1) * tokens] * portion).astype(BF)
                mixed += jnp.dot(qkv_ref[kb, v_rows], probs, preferred_element_type=F32)
            rounded = mixed.astype(BF)
            heads_ref[block, rows] = rounded
            rest_ref[block, rows] = (mixed - rounded.astype(F32)).astype(BF)
            lse_ref[h, block] = jnp.broadcast_to(top + jnp.log(total), (8, tokens))
            return carry

        lax.fori_loop(0, heads_here, one_head, 0)

    context_args = [
        (
            heads_ref.at[block], context_ref.at[quarter], c_send.at[GROUP + block],
            c_recv.at[GROUP + quarter], place, holder(row, block), do,
        )
        for block in range(GROUP)
    ]

    def arrived_mp(r):
        arrived([over_mp(0, r), over_mp(1, r)])

    arrived([over_mp(2, r) for r in range(1, GROUP)])
    start(out_hop(1))
    arrived_mp(1)
    start(both(1, 1))
    for args in x_rest_args:
        send_block(*args)
    attend(0)
    send_block(*context_args[0])
    arrived(out_hop(1))
    start(out_hop(2))
    start([over_mp(i, 2) for i in range(2)])
    attend(1)
    send_block(*context_args[1])
    arrived(both(1, 1))
    start(both(1, 2))
    start([over_mp(i, 3) for i in range(2)])
    attend(2)
    send_block(*context_args[2])
    arrived(out_hop(2))
    start(out_hop(3))
    arrived_mp(2)
    start(both(2, 1))
    attend(3)
    send_block(*context_args[3])
    arrived(both(1, 2))
    start(both(1, 3))
    arrived(both(2, 1))
    start(both(2, 2))
    arrived_mp(3)
    start(both(3, 1))
    for args in g_rest_args:
        send_block(*args)

    attn, middle = big.at[pl.ds(0, width)], big.at[pl.ds(width, width)]
    own_weights = [
        pltpu.make_async_copy(ref, buf.at[0], in_sem.at[i, 0])
        for i, (ref, buf) in enumerate(((up_own, w_up), (down_own, w_down)))
    ]

    def fetch(r, slot):
        return [
            pltpu.make_async_copy(ref.at[:, :, r], buf.at[slot], in_sem.at[i, slot])
            for i, (ref, buf) in enumerate(((up_all, w_up), (down_all, w_down)))
        ]

    start(own_weights)
    rows, lanes = columns // GROUP, width // 2
    arrived(out_hop(3))
    out_loads = [pltpu.make_async_copy(out_own, w_out.at[mp], w_sem.at[0])]
    for r in range(1, GROUP):
        shard = lax.rem(mp + r, GROUP)
        for piece in range(GROUP):
            for side in range(2):
                out_loads.append(
                    pltpu.make_async_copy(
                        out_all.at[piece, side, r],
                        w_out.at[shard, pl.ds(piece * rows, rows), pl.ds(side * lanes, lanes)],
                        w_sem.at[(r * GROUP + piece) * 2 + side],
                    )
                )
    start(out_loads)
    bias_cols = bias_ref[...].T
    for k in range(GROUP):
        pltpu.make_async_copy(grad_ref.at[k], grad_ref.at[k], c_recv.at[k]).wait()

    def cotangent_at(at):
        return grad_ref[:, :, at].reshape(width, 128).astype(F32)

    def centre_grad(at):
        grad = cotangent_at(at)
        gyt[:, at] = (grad - jnp.sum(grad, axis=0, keepdims=True) / width).astype(BF)

    lane_chunks(lanes_count, centre_grad)
    gy[...] = gyt[...].T
    sums_ref[2] = jnp.sum(gy[...].astype(F32), axis=0, keepdims=True)
    for copy in out_loads:
        copy.wait()
    for k in range(GROUP):
        pltpu.make_async_copy(heads_ref.at[k], context_ref.at[k], c_recv.at[GROUP + k]).wait()
    pltpu.make_async_copy(stat_ref, stat_ref, r_recv.at[0]).wait()
    for k in range(GROUP):
        pltpu.make_async_copy(x_more.at[k], x_more.at[k], r_recv.at[1 + k]).wait()
    projected = dot_tn(w_out[0], context_ref[0])
    for s in range(1, GROUP):
        projected += dot_tn(w_out[s], context_ref[s])
    attn[...] = projected + bias_cols[:, 0:1]

    def norm(at):
        values = attn[:, at]
        values = values - jnp.sum(values, axis=0, keepdims=True) / width
        values = jnp.where(final, 0.0, values)
        attn[:, at] = values
        mine = (normed_ref[quarter, :, at].astype(F32) * back_gain[...]) * stat_ref[2:3, at]
        mine = mine + x_more[:, :, at].reshape(width, 128).astype(F32)
        mine = jnp.where(final, 0.0, mine)
        mine_ref[:, at] = mine
        values = values + mine
        middle[:, at] = values
        row_sum = jnp.sum(values, axis=0, keepdims=True)
        square_sum = jnp.sum(values * values, axis=0, keepdims=True)
        inverse = lax.rsqrt((square_sum + row_sum * row_sum) / width + EPS)
        recovered = jnp.where(final, -row_sum, values)
        n2t[:, at] = (recovered * inverse * wide_gain[...]).astype(BF)

    for args in x_rest_args:
        sent_block(*args)
    lane_chunks(lanes_count, norm)
    n2[...] = n2t[...].T
    arrived(both(2, 2))
    start(both(2, 3))
    arrived(both(GROUP - 1, 1))
    start(both(GROUP - 1, 2))
    grads = (
        (d_up, core_up, mine_up, one_up, 1, 2),
        (d_down, core_down, mine_down, one_down, 2, 1),
    )

    def to_sibling(r, slot):
        return [
            remote(g[0].at[slot, :, 1 - di], g[1].at[r], k_send.at[i, slot], k_recv.at[i, r], sibling)
            for i, g in enumerate(grads)
        ]

    def to_column(r):
        copies = []
        for i, g in enumerate(grads):
            first, second = g[4], g[5]
            for n, piece in enumerate((flip(do, first), flip(flip(do, first), second))):
                copies.append(
                    remote(
                        g[2].at[piece, r], g[3].at[n, r], o_send.at[i, n, r], o_recv.at[i, n, r],
                        column(first),
                    )
                )
        return copies

    def combine(r, slot):
        for copy in to_sibling(r, slot):
            copy.wait()
        for g in grads:
            add_pairs(
                GROUP, lambda k: g[2].at[k, r], lambda k: g[0].at[slot, k, di], lambda k: g[1].at[r, k]
            )
        start(to_column(r))

    chunk = 64
    root = 0.7978845608028654

    def shard_step(r, carry):
        slot = lax.rem(r, 2)
        for copy in fetch(r, slot):
            copy.wait()

        @pl.when(r < GROUP - 1)
        def _():
            arrived(both(r + 1, 3))
            start(fetch(r + 1, 1 - slot))

        @pl.when(r == 0)
        def _():
            arrived(both(GROUP - 1, 2))
            start(both(GROUP - 1, 3))

        up = w_up[slot].reshape(width, width)
        down = w_down[slot].reshape(width, width)
        bias = smalls_ref[lax.rem(mp + r, GROUP), 1:2]
        pre[...] = jnp.dot(n2[...], up, preferred_element_type=F32) + bias
        ghid[...] = dot_nt(gy[...], down)

        def gelu(i, carry):
            at = pl.ds(pl.multiple_of(i * chunk, chunk), chunk)
            p = pre[at]
            square = p * p
            t = jnp.tanh(root * (p + 0.044715 * (p * square)))
            half = 0.5 * (1.0 + t)
            hidden[at] = (p * half).astype(BF)
            slope = half + 0.5 * p * (1.0 - t * t) * (root * (1.0 + 3 * 0.044715 * square))
            gpre[at] = (ghid[at] * slope).astype(BF)
            return carry

        lax.fori_loop(0, tokens // chunk, gelu, 0)

        @pl.when(r >= 1)
        def _():
            combine(r - 1, 1 - slot)

        d_down[slot] = dot_tn(hidden[...], gy[...]).astype(BF).reshape(d_down.shape[1:])
        d_up[slot] = (
            jnp.dot(n2t[...], gpre[...], preferred_element_type=F32)
            .astype(BF)
            .reshape(d_up.shape[1:])
        )
        start(to_sibling(r, slot))
        sums_ref[3 + r] = jnp.sum(gpre[...].astype(F32), axis=0, keepdims=True)
        more_mlp = jnp.dot(hidden[...], down, preferred_element_type=F32)
        more_grad = dot_nt(gpre[...], up)

        @pl.when(r == 0)
        def _():
            mlp[...] = more_mlp
            gn2[...] = more_grad

        @pl.when(r > 0)
        def _():
            mlp[...] += more_mlp
            gn2[...] += more_grad

        return carry

    lax.fori_loop(0, GROUP, shard_step, 0)
    combine(GROUP - 1, (GROUP - 1) % 2)
    mlp_y = mlp[...] + bias_ref[1:2]
    pre[...] = mlp_y - jnp.sum(mlp_y, axis=1, keepdims=True) / width
    acc_gain[...] = jnp.zeros_like(acc_gain)
    gat = gyt
    for args in x_args + cot_args + g_rest_args:
        sent_block(*args)
    for k in range(GROUP):
        pltpu.make_async_copy(g_more.at[k], g_more.at[k], r_recv.at[1 + GROUP + k]).wait()

    def back(at):
        mlp_z = jnp.where(final, 0.0, pre[at].T)
        delta = attn[:, at] + mlp_z
        grad = gn2[at].T
        values = middle[:, at]
        row_sum = jnp.sum(values, axis=0, keepdims=True)
        square_sum = jnp.sum(values * values, axis=0, keepdims=True)
        inverse = lax.rsqrt((square_sum + row_sum * row_sum) / width + EPS)
        recovered = jnp.where(final, -row_sum, values)
        acc_gain[...] += grad * recovered * inverse
        scaled = grad * wide_gain[...]
        dot_sum = jnp.sum(scaled * recovered, axis=0, keepdims=True)
        tail = scaled[width - 1 :]
        factor = dot_sum * (inverse * inverse * inverse) / width
        grad_in = inverse * (scaled - tail) - factor * (values + row_sum)
        grad_in = jnp.where(final, 0.0, grad_in)
        gnorm_ref[:, at] = grad_in.astype(BF)
        more = g_more[:, :, at].reshape(width, 128).astype(F32)
        grad_z = jnp.where(final, 0.0, (cotangent_at(at) + more) + grad_in)
        grad_z = grad_z.astype(BF).astype(F32)
        gat[:, at] = (grad_z - jnp.sum(grad_z, axis=0, keepdims=True) / width).astype(BF)
        for j in range(GROUP):
            delta_ref[j, :, at] = delta[j * columns : (j + 1) * columns].astype(BF)

    lane_chunks(lanes_count, back)
    sums_ref[0] = jnp.sum(acc_gain[...].T, axis=0, keepdims=True)
    sums_ref[1] = dot_nt(jnp.ones((8, tokens), BF), gat[...])[:1]
    sums_ref[7] = jnp.zeros_like(sums_ref[7])
    for s in range(GROUP):
        gctx_ref[s] = jnp.dot(w_out[s], gat[...], preferred_element_type=F32).astype(BF)
        terms = dot_nt(context_ref[s], gat[...]).astype(BF)
        for side in range(2):
            dout_ref[:, side, lax.rem(s + GROUP - mp, GROUP)] = terms[
                :, side * lanes : (side + 1) * lanes
            ].reshape(GROUP, rows, lanes)
    sent_block(*head_args)
    for args in context_args:
        sent_block(*args)

    @pl.when(mp == 0)
    def _():
        for args in stat_args:
            sent_block(*args)

    sent = gathers + smalls + heads + sums_over
    for r in range(1, GROUP):
        sent += [over_mp(i, r) for i in range(3)]
        for stage in (1, 2, 3):
            sent += both(r, stage)
    for stage in (1, 2, 3):
        sent += out_hop(stage)
    for copy in sent:
        copy.wait_send()
    for r in range(GROUP):
        for copy in to_column(r):
            copy.wait()


def first_part(stream, cotangent, segment_ids, small, biases, qkv_weight, up, down, out):
    columns, token_count = stream.shape
    width, tokens = columns * GROUP, token_count // GROUP
    heads = columns // HD
    shape = jax.ShapeDtypeStruct
    vmem, anywhere = pl.BlockSpec(memory_space=pltpu.VMEM), pl.BlockSpec(memory_space=pl.ANY)
    dma = pltpu.SemaphoreType.DMA
    up, down = pieces_of(up), pieces_of(down)
    head_pieces = qkv_weight.reshape(GROUP, 3 * columns // GROUP, width)
    slabs = (GROUP, columns, tokens)
    rows = up.shape[2:]
    out_rows = (columns // GROUP, width // 2)
    part, half = (2,) + up.shape, (GROUP, GROUP) + rows
    bf = lambda *dims: pltpu.VMEM(dims, BF)
    fl = lambda *dims: pltpu.VMEM(dims, F32)
    return pl.pallas_call(
        first_kernel,
        out_shape=[
            shape((width, tokens), F32),
            shape(slabs, BF),
            shape(slabs, BF),
            shape((GROUP, 3 * columns, tokens), BF),
            shape((heads, GROUP, 8, tokens), F32),
            shape((GROUP, width, tokens), BF),
            shape((GROUP,) + small.shape, F32),
            shape(head_pieces.shape, BF),
            shape((2, 1, token_count), jnp.int32),
            shape((8, tokens), F32),
            shape(slabs, BF),
            shape(slabs, BF),
            shape((width, tokens), BF),
            shape((8, 1, width), F32),
        ]
        + [shape(half, BF), shape((2,) + half[1:], BF)] * 2
        + [shape((GROUP, 2, GROUP) + out_rows, BF)]
        + [shape((GROUP, 2, GROUP) + p, BF) for p in (rows, rows, out_rows)],
        in_specs=[anywhere] * 2 + [vmem] * 3 + [anywhere] * 4,
        out_specs=[vmem] * 19 + [anywhere] * 3,
        scratch_shapes=[
            bf(*slabs), bf(*slabs), bf(heads, GROUP, tokens, HD),
            fl(token_count, tokens), fl(tokens, tokens), fl(width, 128), fl(width, 128),
            bf(width, tokens), bf(width, tokens), fl(GROUP + 1, GROUP, 8, tokens),
            bf(*slabs), bf(*slabs),
            bf(*part), bf(*part), bf(GROUP, columns, width), bf(*part), bf(*part),
            bf(tokens, width), bf(tokens, width), fl(tokens, width), fl(tokens, width),
            bf(tokens, width), bf(tokens, width), fl(tokens, width), fl(tokens, width),
            fl(width, 128), bf(*half), bf(*half),
            dma((10,)), dma((2, 2)), dma((2 * GROUP * GROUP,)),
            dma((GROUP,)), dma((GROUP,)), dma((3, GROUP)), dma((3, GROUP)),
            dma((2 * GROUP,)), dma((2 * GROUP,)), dma((GROUP,)), dma((GROUP,)),
            dma((GROUP,)), dma((GROUP,)), dma((3 * GROUP,)), dma((1 + 2 * GROUP,)),
            dma((7,)), dma((7,)), dma((3, GROUP)), dma((3, GROUP)),
            dma((2, GROUP, GROUP)), dma((2, GROUP, GROUP)), dma((2, 2)), dma((2, GROUP)),
            dma((2, 2, GROUP)), dma((2, 2, GROUP)),
        ],
        compiler_params=pltpu.CompilerParams(
            collective_id=6, has_side_effects=True, vmem_limit_bytes=62 * 2**20
        ),
    )(stream, cotangent, segment_ids, small, biases, head_pieces, up, down, out)


def local(
    stream, segment_ids, cotangent, ln1_gain, qkv_weight, qv_bias, out_weight, out_bias,
    ln2_gain, up_weight, up_bias, down_weight, down_bias,
):
    columns, token_count = stream.shape
    mp_count = lax.axis_size("mp")
    width = columns * mp_count
    do, di, mp = places()
    row, quarter = mp // 2, own_quarter(di, mp)
    heads_here = columns // HD
    scale = HD ** (-0.5)
    tokens = token_count // GROUP
    keep_local = ((mp * columns + lax.iota(jnp.int32, columns)) != width - 1)[:, None]
    last = (lax.iota(jnp.int32, width) == width - 1)[:, None]

    small = jnp.stack([jnp.concatenate([ln1_gain, ln2_gain, qv_bias[0], qv_bias[1]]), up_bias])
    small = jnp.pad(small, ((0, 6), (0, 0)))
    biases = jnp.pad(jnp.stack([out_bias, down_bias]), ((0, 6), (0, 0)))
    (
        mine, heads_out, heads_rest, qkv, lse, normed_one, smalls, head_weight, segs, stat, delta,
        grad_context, grad_norm_two, sums, *rest,
    ) = first_part(
        stream, cotangent, segment_ids, small, biases, qkv_weight, up_weight, down_weight,
        out_weight,
    )
    weight_grads = rest[:5]
    masked = jnp.where(keep_local, stream, 0.0)
    mixed_in, grad_in_local, qkv_grad, small, up_grad, down_grad, out_grad = backward_part(
        (
            grad_context, delta, mine, grad_norm_two, heads_out, heads_rest, qkv, lse, normed_one,
            smalls, head_weight, segs, stat, sums, *weight_grads,
        )
    )
    local_of = lambda blocks: blocks.transpose(1, 0, 2).reshape(columns, token_count).astype(F32)
    mixed = masked + local_of(mixed_in)
    stream_grad = jnp.where(keep_local, cotangent + local_of(grad_in_local), 0.0)
    qkv_grad = qkv_grad.transpose(0, 2, 1, 3).reshape(3, columns, width)
    up_grad, down_grad = [g.reshape(-1, width) for g in (up_grad, down_grad)]
    out_grad = out_grad.transpose(0, 2, 1, 3).reshape(columns, width)
    if lax.axis_size("blk") > 1:
        small, qkv_grad, up_grad, down_grad, out_grad = lax.psum(
            (small, qkv_grad, up_grad, down_grad, out_grad), "blk"
        )
    small = small[:, 0]
    shard = lambda values: lax.dynamic_slice_in_dim(values, mp * columns, columns, 0)
    at = lambda start, count: lax.dynamic_slice_in_dim(small, start, count, 0)
    return (
        mixed,
        stream_grad,
        shard(small[0]),
        qkv_grad,
        at(8 + 2 * mp, 2)[:, :columns],
        out_grad,
        small[2],
        shard(small[1]),
        up_grad,
        at(4 + mp, 1)[0],
        down_grad,
        small[3],
    )


def solution(mesh):
    rows, mp_count = mesh.shape["dp"], mesh.shape["mp"]
    pairs = Mesh(mesh.devices.reshape(rows // 8, 4, 2, mp_count), ALL)
    return jax.shard_map(
        local,
        mesh=pairs,
        in_specs=(
            P("mp", ROWS),
            P(ROWS, None),
            P("mp", ROWS),
            P("mp"),
            P(None, "mp", None),
            P(None, "mp"),
            P("mp", None),
            P(),
            P("mp"),
            P(None, "mp"),
            P("mp"),
            P("mp", None),
            P(),
        ),
        out_specs=(
            P("mp", ROWS),
            P("mp", ROWS),
            P("mp"),
            P(None, "mp", None),
            P(None, "mp"),
            P("mp", None),
            P(),
            P("mp"),
            P(None, "mp"),
            P("mp"),
            P("mp", None),
            P(),
        ),
        check_vma=False,
    )
```

time: 1020 us -> 321 us (0.31)
  waiting for transfers between devices: 713 us -> 0 us
  Pallas kernels: 0 us -> 293 us
  matrix products: 107 us -> 0 us
  blocking collectives: 82 us -> 0 us
  other arithmetic: 69.1 us -> 7.27 us
  between operations: 16.8 us -> 0.73 us
    reduce_scatter x4 -> x0, waiting for transfers between devices: 396 us -> none  [the longest x2 198 us: branch_out(): summed = lax.psum_scatter(centred, 'mp', scatter_dimension=0, tiled=True)]
    pallas_call x0 -> x2, Pallas kernels: none -> 293 us  [the longest x1 174 us: first_part(): pl.pallas_call(first_kernel, out_shape=[shape((width, tokens), F32), shap...]
    all_gather x4 -> x0, waiting for transfers between devices: 241 us -> none  [the longest x2 123 us: norm_forward(): whole = lax.all_gather(local_rows, 'mp', axis=0, tiled=True)]
    dot_general x36 -> x0, matrix products: 107 us -> none  [the longest x4 11.9 us: local(): jnp.einsum('qhe,khe->hqk', grad_rows, values_in[:end_row], preferred_elem...]
    psum x5 -> x0, blocking collectives: 82 us -> none  [the longest x2 31.3 us: norm_forward(): lax.psum((jnp.sum(values_in, axis=0), jnp.sum(values_in * values_in, axis...]
    psum x1 -> x0, waiting for transfers between devices: 76.4 us -> none  [local(): lax.psum((ln1_grad, qkv_grad, qv_bias_grad, out_grad, out_bias_grad, ln2_...]
    reduce_sum x16 -> x0, other arithmetic: 27.6 us -> none  [the longest x2 6.81 us: norm_backward(): gain_grad = jnp.sum(grad_normed * recovered * inverse[None, :], axis=1)]
    convert_element_type x9 -> x0, other arithmetic: 24.2 us -> none  [the longest x4 13 us: local(): grad_scores = (probs * (grad_probs - weighted)).astype(jnp.bfloat16)]
  transfers between devices with their start and end apart: 9 -> 0, of which waited for: 9 -> 0; matrix products, arithmetic and copies ran while one was open for 7% -> 0% of each run, Pallas kernels for 0% -> 0%
where the time goes in v1:
time: 321 us; the launch traced here: 320 us
  Pallas kernels  293 us (91%)
  local copies, waits for them, and re-layouts  19.1 us (6%)
  other arithmetic  7.27 us (2%)
    pallas_call x1, Pallas kernels, first_part(): pl.pallas_call(first_kernel, out_shape=[shape((width, tokens), F32), shap...  174 us
    pallas_call x1, Pallas kernels, backward_part(): pl.pallas_call(backward_kernel, out_shape=[shape(slabs, BF), shape(slabs,...  119 us

profile of v1, /device:TPU:1, one launch (start us, length us, event | category | flops | bytes accessed | tf_op | source)
XLA Modules:
  0.0 320.2 jit_solution(1247467306256205210)
XLA Ops:
  0.6 0.8 fusion
  1.4 0.8 pad_maximum_fusion
  2.2 0.7 stack.19
  2.9 0.7 stack.21
  3.6 0.7 stack.22
  4.3 0.6 select_maximum_fusion
  4.9 174.4 %shard_map.220 = (f32[768,512]{1,0:T(8,128)}, bf16[4,192,512]{2,1,0:T(8,128)(2,1)}, bf16[4,192,512]{2,1,0:T(8,128)(2,1)}, bf16[4,576,512]{2,1,0:T(8,128)(2,1)}, ...) custom-call(f32[192,2048]{1,0:T(8,128)} %stream_ref.1, ...), custom_call_target="tpu_custom_call" | custom-call | tf_op jit(solution)/shard_map/pallas_call | solution.py:1235
  179.3 118.7 %shard_map.221 = (bf16[4,192,512]{2,1,0:T(8,128)(2,1)}, bf16[4,192,512]{2,1,0:T(8,128)(2,1)}, f32[4,2,144,384]{3,2,1,0:T(8,128)}, f32[16,1,768]{2,1,0:T(1,128)},...) custom-call(bf16[4,192,512]{2,1,0:T(8,128)(2,1)} %get-tuple-element.38.gctx_ref, ...), custom_call_target="tpu_custom_call" | custom-call | tf_op jit(solution)/shard_map/pallas_call | solution.py:552
  298.1 1.3 convert_bitcast_fusion.1
  299.4 1.3 copy.30
  301.0 1.3 copy.31
  302.3 0.6 copy-done
  303.4 4.3 %add_select_fusion = (f32[192,2048]{1,0:T(8,128)}, f32[192,2048]{1,0:T(8,128)}) fusion(f32[192,2048]{1,0:T(8,128)S(1)} %copy-done, f32[192,2048]{1,0:T(8,128)} %bitcast.26, pred[192]{0:T(512)(128)(4,1)S(1)} %add_compare_fusion, f32[192,2048]{1,0:T(8,128)} %bitcast.25, f32[192,2048]{1,0:T(8,128)S(1)} %copy-done.1), kind=kLoop, calls=%fused_computation.2 | loop fusion | flops 1572864 | bytes 9437376 | tf_op jit(solution)/shard_map/jit(_where)/select_n | solution.py:1316
  307.7 0.9 copy.27
  308.6 2.6 reshape.72
  311.6 0.9 copy.32
  312.4 1.3 slice_reduce_fusion
  313.8 0.6 constant_dynamic-slice_fusion
  314.4 0.6 constant_dynamic-slice_fusion.2
  315.0 0.7 constant_dynamic-slice_fusion.1
  315.7 0.6 slice.32
  316.3 1.4 copy.37
  317.7 1.1 copy-done.2
  318.8 1.4 copy.38
  (17 shorter events, 1.0 us)
Async XLA Ops:
  299.4 1.3 copy-start.5
  300.9 2.0 copy-start
  300.9 2.4 copy-start.1
  303.4 4.3 %copy-start.4 = (f32[4,2,144,384]{3,2,1,0:T(8,128)S(1)}, f32[4,2,144,384]{3,2,1,0:T(8,128)}, u32[]{:S(2)}) copy-start(f32[4,2,144,384]{3,2,1,0:T(8,128)} %get-tuple-element.60) | copy-start | bytes 5308420
  308.6 2.6 copy-start.6
  311.3 5.0 %copy-start.3 = (f32[4,2,96,768]{3,2,1,0:T(8,128)S(1)}, f32[4,2,96,768]{3,2,1,0:T(8,128)}, u32[]{:S(2)}) copy-start(f32[4,2,96,768]{3,2,1,0:T(8,128)} %get-tuple-element.62) | copy-start | bytes 7077892
  316.3 2.5 copy-start.2

commit v2 on v1

--- a/solution.py
+++ b/solution.py
@@ -24,7 +24,7 @@
 
 
 def holder(row, quarter):
-    return lax.rem(quarter, 2), 2 * row + quarter // 2
+    return quarter // 2, 2 * row + lax.rem(quarter, 2)
 
 
 def dev(do, di, mp):
@@ -110,9 +110,10 @@
 
 def backward_kernel(
     gctx_ref, delta_ref, x_ref, gn2_ref, heads_ref, rest_ref, qkv_ref, lse_ref, normed_ref,
-    smalls_ref, headw_ref, segs_ref, stat_ref, sums_ref, dup_ref, oup_ref, ddown_ref, odown_ref, dout_ref,
-    m_ref, s_ref, qkvg_ref, small_out, up_out, down_out, out_out,
-    gall, k_tok, v_tok, causal, acc_k, acc_v, gj, acc_w, acc_b, gain_wide, acc_gain,
+    smalls_ref, headw_ref, segs_ref, stat_ref, sums_ref, dup_ref, oup_ref, ddown_ref, odown_ref,
+    dout_ref, stream_ref, cot_ref,
+    small_out, mixed_ref, back_ref, qkvg_ref, up_out, down_out, out_out,
+    s_ref, local_in, m_in, gall, k_tok, v_tok, causal, acc_k, acc_v, gj, acc_w, acc_b, gain_wide, acc_gain,
     part, near, total, far_buf, s_blocks,
     core_out, mine_up, mine_down, mine_out,
     one_up, one_down, one_out, two_up, two_down, two_out, z_up, z_down, z_out,
@@ -162,6 +163,8 @@
             own.append(pltpu.make_async_copy(g[0].at[piece], g[1].at[piece], own_sem.at[4 + 2 * i + n]))
         own.append(pltpu.make_async_copy(g[2], g[3], own_sem.at[8 + i]))
     own.append(pltpu.make_async_copy(dout_ref.at[:, di], mine_out, own_sem.at[2]))
+    mixed_load = pltpu.make_async_copy(stream_ref, local_in, own_sem.at[10])
+    mixed_load.start()
     for copy in own:
         copy.start()
     greet(neighbours(do, di, mp))
@@ -238,31 +241,31 @@
         part[block] = dot_tn(head_weight, gj[...])
 
     def near_args(i):
-        return part.at[i], near.at[i // 2], r_send.at[i], r_recv.at[i], sibling
+        return part.at[i], near.at[i % 2], r_send.at[i], r_recv.at[i], sibling
 
     def far_args(i):
         return total, far_buf, r_send.at[GROUP + i], r_recv.at[GROUP + i], across
 
     def to_sibling(i):
-        @pl.when(di != i % 2)
+        @pl.when(di != i // 2)
         def _():
             remote(*near_args(i)).start()
 
     def across_row(i):
-        @pl.when(di == i % 2)
+        @pl.when(di == i // 2)
         def _():
             remote(*near_args(i)).wait_recv()
             at = lambda k: pl.ds(pl.multiple_of(k * columns, columns), columns)
             add_pairs(
                 GROUP,
-                lambda k: near.at[i // 2, at(k)],
-                lambda k: near.at[i // 2, at(k)],
+                lambda k: near.at[i % 2, at(k)],
+                lambda k: near.at[i % 2, at(k)],
                 lambda k: part.at[i, at(k)],
             )
 
-            @pl.when(half != i // 2)
+            @pl.when(half != i % 2)
             def _():
-                total[...] = near[i // 2].astype(BF)
+                total[...] = near[i % 2].astype(BF)
                 remote(*far_args(i)).start()
 
     def weight_terms(block):
@@ -312,6 +315,9 @@
                 )
         return later
 
+    def result_of(i, piece):
+        return grads[i][7].at[piece, di] if i < 2 else piece_of(out_out, piece, di)
+
     def stage_four(copies):
         arrived(copies)
         later = []
@@ -321,32 +327,51 @@
                 mine[do, 0].astype(F32) + z_buf[0].astype(F32)
                 + z_buf[1].astype(F32) + z_buf[2].astype(F32)
             )
-            pltpu.make_async_copy(fin, g[7].at[do, di], own_sem.at[i]).start()
-            later.append(post(fin, g[7].at[do, di], column(g[8])))
+            target = result_of(i, do)
+            pltpu.make_async_copy(fin, target, own_sem.at[i]).start()
+            later.append(post(fin, target, column(g[8])))
         return later
 
     def stage_five(copies):
         arrived(copies)
         later = []
         for i, g in enumerate(grads):
-            pltpu.make_async_copy(g[6], g[7].at[do, di], own_sem.at[i]).wait()
+            pltpu.make_async_copy(g[6], result_of(i, do), own_sem.at[i]).wait()
             for piece in (do, flip(do, g[8])):
-                later.append(post(g[7].at[piece, di], g[7].at[piece, di], column(g[9])))
+                later.append(post(result_of(i, piece), result_of(i, piece), column(g[9])))
         return later
 
     def stage_six(copies):
         arrived(copies)
-        return [post(g[7].at[:, di], g[7].at[:, di], sibling) for g in grads]
+        halves = [g[7].at[:, di] for g in grads[:2]]
+        lanes = out_out.shape[1] // 2
+        halves.append(out_out.at[:, pl.ds(pl.multiple_of(di * lanes, lanes), lanes)])
+        return [post(h, h, sibling) for h in halves]
 
     for copy in own[:-1]:
         copy.wait()
     copies = stage_two(grads[:2])
+    not_last = jnp.logical_or(
+        mp < GROUP - 1, lax.broadcasted_iota(jnp.int32, (columns, 128), 0) < columns - 1
+    )
+
+    def add_local(blocks):
+        def step(n, carry):
+            k, lane = n // (tokens // 128), lax.rem(n, tokens // 128)
+            at = pl.ds(pl.multiple_of(n * 128, 128), 128)
+            inner = pl.ds(pl.multiple_of(lane * 128, 128), 128)
+            value = local_in[:, at] + blocks[k, :, inner].astype(F32)
+            local_in[:, at] = jnp.where(not_last, value, 0.0)
+            return carry
+
+        lax.fori_loop(0, GROUP * (tokens // 128), step, 0)
+
     for k in range(GROUP):
         pltpu.make_async_copy(gctx_ref.at[k], gall.at[k], b_recv.at[k]).wait()
     for k in range(GROUP):
         swaps.append(
             (
-                delta_ref.at[k], m_ref.at[quarter], b_send.at[GROUP + k],
+                delta_ref.at[k], m_in.at[quarter], b_send.at[GROUP + k],
                 b_recv.at[GROUP + quarter], place, (row, k), do,
             )
         )
@@ -367,6 +392,12 @@
     across_row(2)
     weight_terms(1)
     copies += stage_three(out_copies, grads[2:])
+    for k in range(GROUP):
+        pltpu.make_async_copy(delta_ref.at[k], m_in.at[k], b_recv.at[GROUP + k]).wait()
+    mixed_load.wait()
+    add_local(m_in)
+    mixed_out = pltpu.make_async_copy(local_in, mixed_ref, own_sem.at[10])
+    mixed_out.start()
     back_block(0)
     to_sibling(0)
     across_row(1)
@@ -381,19 +412,18 @@
     for side, (first, second) in enumerate(bits):
         for n, piece in enumerate((flip(do, first), flip(flip(do, first), second))):
             q_copies.append(post(gq.at[piece, :, sides[side]], q_one.at[side, n], column(first)))
-    copies = stage_four(copies)
 
     @pl.when(half == 0)
     def _():
-        for i in (0, 1):
-            @pl.when(di == i)
+        for i in (0, 2):
+            @pl.when(di == i // 2)
             def _():
                 remote(*far_args(i)).wait_recv()
 
     @pl.when(half == 1)
     def _():
-        for i in (2, 3):
-            @pl.when(di == i - 2)
+        for i in (1, 3):
+            @pl.when(di == i // 2)
             def _():
                 remote(*far_args(i)).wait_recv()
 
@@ -426,6 +456,9 @@
             )
         )
         send_block(*swaps[2 * GROUP + k])
+    mixed_out.wait()
+    cot_load = pltpu.make_async_copy(cot_ref, local_in, own_sem.at[11])
+    cot_load.start()
 
     small_a[...] = jnp.zeros_like(small_a)
     small_a[0] = jnp.sum(acc_gain[...].T, axis=0, keepdims=True)
@@ -439,6 +472,7 @@
     small_one = post(small_a, small_b.at[0], sibling)
 
     arrived(q_copies)
+    copies = stage_four(copies)
     q_copies = []
     for side, (first, second) in enumerate(bits):
         for n, piece in ((1, flip(do, second)), (0, do)):
@@ -473,7 +507,11 @@
     q_fin[...] = q_z[0].astype(F32) + q_z[1].astype(F32)
 
     def q_ref(piece, core):
-        return qkvg_ref.at[piece, core]
+        count = gq.shape[1]
+        return qkvg_ref.at[
+            pl.ds(pl.multiple_of(piece * count, count), count),
+            pl.ds(pl.multiple_of(core * wide, wide), wide),
+        ]
 
     q_own = pltpu.make_async_copy(q_fin, q_ref(do, di), own_sem.at[3])
     q_own.start()
@@ -502,34 +540,39 @@
 
     q_own.wait()
     q_last.wait_recv()
-    q_copies = [post(qkvg_ref.at[:, di], qkvg_ref.at[:, di], sibling)]
+    q_half = qkvg_ref.at[:, pl.ds(pl.multiple_of(di * wide, wide), wide)]
+    q_copies = [post(q_half, q_half, sibling)]
     arrived(small_copies)
     small_out[...] = small_z[0] + small_z[1] + small_z[2] + small_z[3]
     arrived(q_copies)
 
     for k in range(GROUP):
-        pltpu.make_async_copy(delta_ref.at[k], m_ref.at[k], b_recv.at[GROUP + k]).wait()
         pltpu.make_async_copy(s_blocks.at[k], s_ref.at[k], b_recv.at[2 * GROUP + k]).wait()
+    cot_load.wait()
+    add_local(s_ref)
+    back_out = pltpu.make_async_copy(local_in, back_ref, own_sem.at[11])
+    back_out.start()
     for args in swaps + z_args:
         sent_block(*args)
     for i in range(GROUP):
-        @pl.when(di != i % 2)
+        @pl.when(di != i // 2)
         def _():
             remote(*near_args(i)).wait_send()
 
-        @pl.when(jnp.logical_and(di == i % 2, half != i // 2))
+        @pl.when(jnp.logical_and(di == i // 2, half != i % 2))
         def _():
             remote(*far_args(i)).wait_send()
 
     arrived(copies)
     for copy in pending:
         copy.wait_send()
+    back_out.wait()
 
 
 def backward_part(values):
     (
-        grad_context, delta, x_mine, grad_norm, heads_out, _, qkv, lse, normed, smalls,
-        head_weight, segs, _, sums, up_grad, _, down_grad, _, out_grad,
+        grad_context, _, x_mine, grad_norm, heads_out, _, qkv, lse, normed, smalls,
+        head_weight, segs, _, sums, up_grad, _, down_grad, _, out_grad, stream, _,
     ) = values
     columns, tokens = heads_out.shape[1:]
     width = x_mine.shape[0]
@@ -552,15 +595,19 @@
     return pl.pallas_call(
         backward_kernel,
         out_shape=[
-            shape(slabs, BF),
-            shape(slabs, BF),
-            shape((GROUP, 2, pieces, width // 2), F32),
             shape((16, 1, width), F32),
+            shape(stream.shape, F32),
+            shape(stream.shape, F32),
+            shape((GROUP * pieces, width), F32),
         ]
-        + [shape((GROUP, 2) + r, F32) for r in rows],
-        in_specs=[vmem] * 14 + [anywhere] * 5,
-        out_specs=[vmem] * 4 + [anywhere] * 3,
+        + [shape((GROUP, 2) + r, F32) for r in rows[:2]]
+        + [shape((columns, width), F32)],
+        in_specs=[vmem] * 14 + [anywhere] * 7,
+        out_specs=[vmem] + [anywhere] * 6,
         scratch_shapes=[
+            pltpu.VMEM(slabs, BF),
+            pltpu.VMEM(stream.shape, F32),
+            pltpu.VMEM(slabs, BF),
             pltpu.VMEM(slabs, BF),
             pltpu.VMEM((heads, GROUP, tokens, HD), BF),
             pltpu.VMEM((heads, GROUP, tokens, HD), BF),
@@ -589,7 +636,7 @@
             pltpu.VMEM((16, 1, width), F32),
             pltpu.VMEM((3, 16, 1, width), F32),
             pltpu.VMEM((GROUP, 16, 1, width), F32),
-            dma((10,)),
+            dma((12,)),
             dma((14,)),
             dma((14,)),
             dma((2 * GROUP,)),
@@ -604,7 +651,7 @@
 
 
 def own_quarter(di, mp):
-    return 2 * lax.rem(mp, 2) + di
+    return 2 * di + lax.rem(mp, 2)
 
 
 def lane_chunks(count, step):
@@ -621,7 +668,8 @@
 
 
 def first_kernel(
-    stream_ref, cot_ref, seg_ref, small_ref, bias_ref, qkvw_ref, up_own, down_own, out_own,
+    stream_ref, cot_ref, seg_ref, gain1_ref, gain2_ref, qv_ref, upb_ref, outb_ref, downb_ref,
+    qkvw_ref, up_own, down_own, out_own,
     mine_ref, heads_ref, rest_ref, qkv_ref, lse_ref, normed_ref, smalls_ref, headw_ref, segs_ref,
     stat_ref, delta_ref, gctx_ref, gnorm_ref, sums_ref, mine_up, one_up, mine_down, one_down, dout_ref,
     up_all, down_all, out_all,
@@ -640,7 +688,7 @@
     row, quarter = mp // 2, own_quarter(di, mp)
     place = (di, mp)
     sibling, across = dev(do, 1 - di, mp), dev(do, di, flip(mp, 1))
-    far = 2 * (1 - lax.rem(mp, 2)) + di
+    far = 2 * di + 1 - lax.rem(mp, 2)
     weights = ((up_own, up_all), (down_own, down_all), (out_own, out_all))
     final = lax.broadcasted_iota(jnp.int32, (width, 128), 0) == width - 1
 
@@ -657,25 +705,79 @@
                     own_sem.at[2 + GROUP * i + k],
                 )
             )
-    own = [
-        pltpu.make_async_copy(small_ref, smalls_ref.at[mp], own_sem.at[0]),
-        pltpu.make_async_copy(seg_ref, segs_ref.at[di], own_sem.at[1]),
-    ]
+    own = [pltpu.make_async_copy(seg_ref, segs_ref.at[di], own_sem.at[1])]
     for copy in loads + own:
         copy.start()
+    smalls_ref[mp] = jnp.zeros(smalls_ref.shape[1:], F32)
+    smalls_ref[mp, 0:1, :columns] = gain1_ref[...]
+    smalls_ref[mp, 1:2, :columns] = gain2_ref[...]
+    smalls_ref[mp, 2:4, :columns] = qv_ref[...]
+    smalls_ref[mp, 4:5] = upb_ref[...]
     greet(neighbours(do, di, mp))
     is_last = jnp.logical_and(
         mp == GROUP - 1, lax.broadcasted_iota(jnp.int32, (columns, tokens), 0) == columns - 1
     )
 
     def target_of(k):
-        return lax.rem(k, 2), 2 * di + k // 2
+        return k // 2, 2 * di + k % 2
 
     def rows_at(j):
         return pl.ds(pl.multiple_of(j * columns, 64), columns)
 
     def others():
         return [dev(do, di, lax.rem(mp + r, GROUP)) for r in range(1, GROUP)]
+
+    def over_mp(i, r):
+        ref, all_ref = weights[i]
+        return remote(
+            ref.at[do, di] if i < 2 else piece_of(ref, do, di), all_ref.at[do, di, r],
+            a_send.at[i, r], a_recv.at[i, r], dev(do, di, lax.rem(mp + GROUP - r, GROUP)),
+        )
+
+    orders = ((1, 2), (2, 1))
+
+    def hop(i, r, stage):
+        all_ref = weights[i][1]
+        first, second = orders[i]
+        if stage == 3:
+            ref = all_ref.at[:, di, r]
+            return [remote(ref, ref, t_send.at[i, r, 3], t_recv.at[i, r, 3], sibling)]
+        pieces = (do,) if stage == 1 else (do, flip(do, first))
+        bit = first if stage == 1 else second
+        copies = []
+        for n, piece in enumerate(pieces):
+            ref = all_ref.at[piece, di, r]
+            at = stage - 1 + n
+            copies.append(remote(ref, ref, t_send.at[i, r, at], t_recv.at[i, r, at], column(bit)))
+        return copies
+
+    def out_hop(stage):
+        if stage == 3:
+            ref = out_all.at[:, di, pl.ds(1, GROUP - 1)]
+            return [remote(ref, ref, t_send.at[0, 0, 3], t_recv.at[0, 0, 3], sibling)]
+        pieces = (do,) if stage == 1 else (do, flip(do, 1))
+        copies = []
+        for n, piece in enumerate(pieces):
+            ref = out_all.at[piece, di, pl.ds(1, GROUP - 1)]
+            at = stage - 1 + n
+            copies.append(
+                remote(ref, ref, t_send.at[0, 0, at], t_recv.at[0, 0, at], column(stage))
+            )
+        return copies
+
+    def start(copies):
+        for copy in copies:
+            copy.start()
+
+    def arrived(copies):
+        for copy in copies:
+            copy.wait_recv()
+
+    def arrived_mp(r):
+        arrived([over_mp(0, r), over_mp(1, r)])
+
+    def both(r, stage):
+        return hop(0, r, stage) + hop(1, r, stage)
 
     x_rest = [n2t.at[pl.ds(k * columns, columns)] for k in range(GROUP)]
     g_rest = [gnorm_ref.at[pl.ds(k * columns, columns)] for k in range(GROUP)]
@@ -697,13 +799,12 @@
     for r in range(1, GROUP):
         target = dev(do, di, lax.rem(mp + r, GROUP))
         smalls.append(
-            remote(small_ref, smalls_ref.at[mp], s_send.at[r], s_recv.at[GROUP - r], target)
+            remote(smalls_ref.at[mp], smalls_ref.at[mp], s_send.at[r], s_recv.at[GROUP - r], target)
         )
     smalls.append(remote(seg_ref, segs_ref.at[di], s_send.at[0], s_recv.at[0], sibling))
     for copy in smalls:
         copy.start()
-    own_turned = small_ref[...].T
-    own_gain = own_turned[:columns, 0:1]
+    own_gain = smalls_ref[mp].T[:columns, 0:1]
     for copy in sums_over:
         copy.wait_recv()
     x_args, stat_args, x_rest_args = [], [], []
@@ -743,7 +844,7 @@
         for args in stat_args:
             send_block(*args)
 
-    head_target = (lax.rem(mp, 2), mp // 2 + 2 * di)
+    head_target = (mp // 2, lax.rem(mp, 2) + 2 * di)
     head_args = (
         qkvw_ref.at[do], headw_ref.at[do], h_send.at[0], h_recv.at[0], place, head_target, do,
     )
@@ -759,59 +860,8 @@
             copy.start()
             gathers.append(copy)
 
-    def over_mp(i, r):
-        ref, all_ref = weights[i]
-        return remote(
-            ref.at[do, di] if i < 2 else piece_of(ref, do, di), all_ref.at[do, di, r],
-            a_send.at[i, r], a_recv.at[i, r], dev(do, di, lax.rem(mp + GROUP - r, GROUP)),
-        )
-
-    for r in range(1, GROUP):
-        over_mp(2, r).start()
-    for i in range(2):
-        over_mp(i, 1).start()
-
-    orders = ((1, 2), (2, 1))
-
-    def hop(i, r, stage):
-        all_ref = weights[i][1]
-        first, second = orders[i]
-        if stage == 3:
-            ref = all_ref.at[:, di, r]
-            return [remote(ref, ref, t_send.at[i, r, 3], t_recv.at[i, r, 3], sibling)]
-        pieces = (do,) if stage == 1 else (do, flip(do, first))
-        bit = first if stage == 1 else second
-        copies = []
-        for n, piece in enumerate(pieces):
-            ref = all_ref.at[piece, di, r]
-            at = stage - 1 + n
-            copies.append(remote(ref, ref, t_send.at[i, r, at], t_recv.at[i, r, at], column(bit)))
-        return copies
-
-    def out_hop(stage):
-        if stage == 3:
-            ref = out_all.at[:, di, pl.ds(1, GROUP - 1)]
-            return [remote(ref, ref, t_send.at[0, 0, 3], t_recv.at[0, 0, 3], sibling)]
-        pieces = (do,) if stage == 1 else (do, flip(do, 1))
-        copies = []
-        for n, piece in enumerate(pieces):
-            ref = out_all.at[piece, di, pl.ds(1, GROUP - 1)]
-            at = stage - 1 + n
-            copies.append(
-                remote(ref, ref, t_send.at[0, 0, at], t_recv.at[0, 0, at], column(stage))
-            )
-        return copies
-
-    def start(copies):
-        for copy in copies:
-            copy.start()
-
-    def arrived(copies):
-        for copy in copies:
-            copy.wait_recv()
-
-    def both(r, stage):
-        return hop(0, r, stage) + hop(1, r, stage)
+    start([over_mp(2, r) for r in range(1, GROUP)])
+    start([over_mp(i, r) for r in (1, 2) for i in range(2)])
 
     pltpu.make_async_copy(qkvw_ref.at[do], headw_ref.at[do], h_recv.at[0]).wait()
     cut = 80
@@ -835,10 +885,9 @@
         turned = smalls_ref[j].T
         at = slice(j * columns, (j + 1) * columns)
         back_gain[at] = jnp.broadcast_to(1.0 / turned[:columns, 0:1], (columns, 128))
-        wide_gain[at] = jnp.broadcast_to(turned[columns : 2 * columns, 0:1], (columns, 128))
+        wide_gain[at] = jnp.broadcast_to(turned[:columns, 1:2], (columns, 128))
     biases = smalls_ref[quarter].T
-    query_bias = biases[2 * columns : 3 * columns, 0:1]
-    value_bias = biases[3 * columns :, 0:1]
+    query_bias, value_bias = biases[:columns, 2:3], biases[:columns, 3:4]
     causal[...] = jnp.where(
         lax.broadcasted_iota(jnp.int32, causal.shape, 0)
         <= lax.broadcasted_iota(jnp.int32, causal.shape, 1),
@@ -868,8 +917,12 @@
         (gctx_ref.at[k], grad_ref.at[mp], c_send.at[k], c_recv.at[mp], place, target_of(k), do)
         for k in range(GROUP)
     ]
-    for args in cot_args:
+    for args in x_rest_args:
         send_block(*args)
+    arrived([over_mp(2, r) for r in range(1, GROUP)])
+    start(out_hop(1))
+    arrived_mp(1)
+    start(both(1, 1))
     g_rest_args = [
         (
             g_rest[k], g_more.at[mp], r_send.at[2 * GROUP + k], r_recv.at[1 + GROUP + mp],
@@ -936,39 +989,31 @@
         for block in range(GROUP)
     ]
 
-    def arrived_mp(r):
-        arrived([over_mp(0, r), over_mp(1, r)])
-
-    arrived([over_mp(2, r) for r in range(1, GROUP)])
-    start(out_hop(1))
-    arrived_mp(1)
-    start(both(1, 1))
-    for args in x_rest_args:
-        send_block(*args)
     attend(0)
     send_block(*context_args[0])
+    for args in cot_args:
+        send_block(*args)
     arrived(out_hop(1))
     start(out_hop(2))
-    start([over_mp(i, 2) for i in range(2)])
+    arrived_mp(2)
+    start(both(2, 1))
+    arrived(both(1, 1))
+    start(both(1, 2))
     attend(1)
     send_block(*context_args[1])
-    arrived(both(1, 1))
-    start(both(1, 2))
     start([over_mp(i, 3) for i in range(2)])
     attend(2)
     send_block(*context_args[2])
     arrived(out_hop(2))
     start(out_hop(3))
-    arrived_mp(2)
-    start(both(2, 1))
-    attend(3)
-    send_block(*context_args[3])
     arrived(both(1, 2))
     start(both(1, 3))
     arrived(both(2, 1))
     start(both(2, 2))
-    arrived_mp(3)
-    start(both(3, 1))
+    attend(3)
+    send_block(*context_args[3])
+    arrived(both(2, 2))
+    start(both(2, 3))
     for args in g_rest_args:
         send_block(*args)
 
@@ -1000,10 +1045,7 @@
                     )
                 )
     start(out_loads)
-    bias_cols = bias_ref[...].T
-    for k in range(GROUP):
-        pltpu.make_async_copy(grad_ref.at[k], grad_ref.at[k], c_recv.at[k]).wait()
-
+    out_bias = jnp.broadcast_to(outb_ref[...], (8, width)).T[:, 0:1]
     def cotangent_at(at):
         return grad_ref[:, :, at].reshape(width, 128).astype(F32)
 
@@ -1011,9 +1053,6 @@
         grad = cotangent_at(at)
         gyt[:, at] = (grad - jnp.sum(grad, axis=0, keepdims=True) / width).astype(BF)
 
-    lane_chunks(lanes_count, centre_grad)
-    gy[...] = gyt[...].T
-    sums_ref[2] = jnp.sum(gy[...].astype(F32), axis=0, keepdims=True)
     for copy in out_loads:
         copy.wait()
     for k in range(GROUP):
@@ -1024,7 +1063,7 @@
     projected = dot_tn(w_out[0], context_ref[0])
     for s in range(1, GROUP):
         projected += dot_tn(w_out[s], context_ref[s])
-    attn[...] = projected + bias_cols[:, 0:1]
+    attn[...] = projected + out_bias
 
     def norm(at):
         values = attn[:, at]
@@ -1047,10 +1086,14 @@
         sent_block(*args)
     lane_chunks(lanes_count, norm)
     n2[...] = n2t[...].T
-    arrived(both(2, 2))
-    start(both(2, 3))
-    arrived(both(GROUP - 1, 1))
-    start(both(GROUP - 1, 2))
+    for k in range(GROUP):
+        pltpu.make_async_copy(grad_ref.at[k], grad_ref.at[k], c_recv.at[k]).wait()
+
+    lane_chunks(lanes_count, centre_grad)
+    gy[...] = gyt[...].T
+    sums_ref[2] = jnp.sum(gy[...].astype(F32), axis=0, keepdims=True)
+    arrived_mp(GROUP - 1)
+    start(both(GROUP - 1, 1))
     grads = (
         (d_up, core_up, mine_up, one_up, 1, 2),
         (d_down, core_down, mine_down, one_down, 2, 1),
@@ -1097,16 +1140,18 @@
             arrived(both(r + 1, 3))
             start(fetch(r + 1, 1 - slot))
 
-        @pl.when(r == 0)
-        def _():
-            arrived(both(GROUP - 1, 2))
-            start(both(GROUP - 1, 3))
-
         up = w_up[slot].reshape(width, width)
         down = w_down[slot].reshape(width, width)
-        bias = smalls_ref[lax.rem(mp + r, GROUP), 1:2]
+        bias = smalls_ref[lax.rem(mp + r, GROUP), 4:5]
         pre[...] = jnp.dot(n2[...], up, preferred_element_type=F32) + bias
         ghid[...] = dot_nt(gy[...], down)
+
+        for step in (0, 1):
+
+            @pl.when(r == step)
+            def _():
+                arrived(both(GROUP - 1, 1 + step))
+                start(both(GROUP - 1, 2 + step))
 
         def gelu(i, carry):
             at = pl.ds(pl.multiple_of(i * chunk, chunk), chunk)
@@ -1150,18 +1195,25 @@
 
     lax.fori_loop(0, GROUP, shard_step, 0)
     combine(GROUP - 1, (GROUP - 1) % 2)
-    mlp_y = mlp[...] + bias_ref[1:2]
+    for args in x_args:
+        sent_block(*args)
+    mlp_y = mlp[...] + downb_ref[...]
     pre[...] = mlp_y - jnp.sum(mlp_y, axis=1, keepdims=True) / width
+
+    def mixed_delta(at):
+        delta = attn[:, at] + jnp.where(final, 0.0, pre[at].T)
+        for j in range(GROUP):
+            delta_ref[j, :, at] = delta[j * columns : (j + 1) * columns].astype(BF)
+
+    lane_chunks(lanes_count, mixed_delta)
     acc_gain[...] = jnp.zeros_like(acc_gain)
     gat = gyt
-    for args in x_args + cot_args + g_rest_args:
+    for args in cot_args + g_rest_args:
         sent_block(*args)
     for k in range(GROUP):
         pltpu.make_async_copy(g_more.at[k], g_more.at[k], r_recv.at[1 + GROUP + k]).wait()
 
     def back(at):
-        mlp_z = jnp.where(final, 0.0, pre[at].T)
-        delta = attn[:, at] + mlp_z
         grad = gn2[at].T
         values = middle[:, at]
         row_sum = jnp.sum(values, axis=0, keepdims=True)
@@ -1180,8 +1232,6 @@
         grad_z = jnp.where(final, 0.0, (cotangent_at(at) + more) + grad_in)
         grad_z = grad_z.astype(BF).astype(F32)
         gat[:, at] = (grad_z - jnp.sum(grad_z, axis=0, keepdims=True) / width).astype(BF)
-        for j in range(GROUP):
-            delta_ref[j, :, at] = delta[j * columns : (j + 1) * columns].astype(BF)
 
     lane_chunks(lanes_count, back)
     sums_ref[0] = jnp.sum(acc_gain[...].T, axis=0, keepdims=True)
@@ -1217,7 +1267,7 @@
             copy.wait()
 
 
-def first_part(stream, cotangent, segment_ids, small, biases, qkv_weight, up, down, out):
+def first_part(stream, cotangent, segment_ids, smalls, qkv_weight, up, down, out):
     columns, token_count = stream.shape
     width, tokens = columns * GROUP, token_count // GROUP
     heads = columns // HD
@@ -1241,7 +1291,7 @@
             shape((GROUP, 3 * columns, tokens), BF),
             shape((heads, GROUP, 8, tokens), F32),
             shape((GROUP, width, tokens), BF),
-            shape((GROUP,) + small.shape, F32),
+            shape((GROUP, 8, width), F32),
             shape(head_pieces.shape, BF),
             shape((2, 1, token_count), jnp.int32),
             shape((8, tokens), F32),
@@ -1253,7 +1303,7 @@
         + [shape(half, BF), shape((2,) + half[1:], BF)] * 2
         + [shape((GROUP, 2, GROUP) + out_rows, BF)]
         + [shape((GROUP, 2, GROUP) + p, BF) for p in (rows, rows, out_rows)],
-        in_specs=[anywhere] * 2 + [vmem] * 3 + [anywhere] * 4,
+        in_specs=[anywhere] * 2 + [vmem] * 7 + [anywhere] * 4,
         out_specs=[vmem] * 19 + [anywhere] * 3,
         scratch_shapes=[
             bf(*slabs), bf(*slabs), bf(heads, GROUP, tokens, HD),
@@ -1267,7 +1317,7 @@
             dma((10,)), dma((2, 2)), dma((2 * GROUP * GROUP,)),
             dma((GROUP,)), dma((GROUP,)), dma((3, GROUP)), dma((3, GROUP)),
             dma((2 * GROUP,)), dma((2 * GROUP,)), dma((GROUP,)), dma((GROUP,)),
-            dma((GROUP,)), dma((GROUP,)), dma((3 * GROUP,)), dma((1 + 2 * GROUP,)),
+            dma((GROUP,)), dma((GROUP,)), dma((4 * GROUP,)), dma((1 + 3 * GROUP,)),
             dma((7,)), dma((7,)), dma((3, GROUP)), dma((3, GROUP)),
             dma((2, GROUP, GROUP)), dma((2, GROUP, GROUP)), dma((2, 2)), dma((2, GROUP)),
             dma((2, 2, GROUP)), dma((2, 2, GROUP)),
@@ -1275,48 +1325,34 @@
         compiler_params=pltpu.CompilerParams(
             collective_id=6, has_side_effects=True, vmem_limit_bytes=62 * 2**20
         ),
-    )(stream, cotangent, segment_ids, small, biases, head_pieces, up, down, out)
+    )(stream, cotangent, segment_ids, *smalls, head_pieces, up, down, out)
 
 
 def local(
     stream, segment_ids, cotangent, ln1_gain, qkv_weight, qv_bias, out_weight, out_bias,
     ln2_gain, up_weight, up_bias, down_weight, down_bias,
 ):
-    columns, token_count = stream.shape
-    mp_count = lax.axis_size("mp")
-    width = columns * mp_count
-    do, di, mp = places()
-    row, quarter = mp // 2, own_quarter(di, mp)
-    heads_here = columns // HD
-    scale = HD ** (-0.5)
-    tokens = token_count // GROUP
-    keep_local = ((mp * columns + lax.iota(jnp.int32, columns)) != width - 1)[:, None]
-    last = (lax.iota(jnp.int32, width) == width - 1)[:, None]
-
-    small = jnp.stack([jnp.concatenate([ln1_gain, ln2_gain, qv_bias[0], qv_bias[1]]), up_bias])
-    small = jnp.pad(small, ((0, 6), (0, 0)))
-    biases = jnp.pad(jnp.stack([out_bias, down_bias]), ((0, 6), (0, 0)))
+    columns = stream.shape[0]
+    mp = lax.axis_index("mp")
+    smalls_in = [
+        ln1_gain[None], ln2_gain[None], qv_bias, up_bias[None], out_bias[None], down_bias[None]
+    ]
     (
-        mine, heads_out, heads_rest, qkv, lse, normed_one, smalls, head_weight, segs, stat, delta,
-        grad_context, grad_norm_two, sums, *rest,
+        mine, heads_out, heads_rest, qkv, lse, normed_one, smalls, head_weight, segs, stat,
+        delta, grad_context, grad_norm_two, sums, *rest,
     ) = first_part(
-        stream, cotangent, segment_ids, small, biases, qkv_weight, up_weight, down_weight,
-        out_weight,
+        stream, cotangent, segment_ids, smalls_in, qkv_weight, up_weight, down_weight, out_weight
     )
     weight_grads = rest[:5]
-    masked = jnp.where(keep_local, stream, 0.0)
-    mixed_in, grad_in_local, qkv_grad, small, up_grad, down_grad, out_grad = backward_part(
+    small, mixed, stream_grad, qkv_grad, up_grad, down_grad, out_grad = backward_part(
         (
             grad_context, delta, mine, grad_norm_two, heads_out, heads_rest, qkv, lse, normed_one,
-            smalls, head_weight, segs, stat, sums, *weight_grads,
+            smalls, head_weight, segs, stat, sums, *weight_grads, stream, cotangent,
         )
     )
-    local_of = lambda blocks: blocks.transpose(1, 0, 2).reshape(columns, token_count).astype(F32)
-    mixed = masked + local_of(mixed_in)
-    stream_grad = jnp.where(keep_local, cotangent + local_of(grad_in_local), 0.0)
-    qkv_grad = qkv_grad.transpose(0, 2, 1, 3).reshape(3, columns, width)
+    width = small.shape[-1]
+    qkv_grad = qkv_grad.reshape(3, columns, width)
     up_grad, down_grad = [g.reshape(-1, width) for g in (up_grad, down_grad)]
-    out_grad = out_grad.transpose(0, 2, 1, 3).reshape(columns, width)
     if lax.axis_size("blk") > 1:
         small, qkv_grad, up_grad, down_grad, out_grad = lax.psum(
             (small, qkv_grad, up_grad, down_grad, out_grad), "blk"

time: 321 us -> 298 us (0.928)
  Pallas kernels: 293 us -> 278 us
  other arithmetic: 7.27 us -> 0 us
    pallas_call x1, Pallas kernels: 174 us -> 158 us  [first_part(): pl.pallas_call(first_kernel, out_shape=[shape((width, tokens), F32), shap...]
    unnamed x18 -> x17, local copies, waits for them, and re-layouts: 5.92 us -> 11.5 us
    select_n x1 -> x0, other arithmetic: 4.33 us -> none  [local(): jnp.where(keep_local, cotangent + local_of(grad_in_local), 0.0)]
    broadcast_in_dim x0 -> x3, local copies, waits for them, and re-layouts: none -> 3.8 us  [the longest x1 1.27 us: local(): up_bias[None]]
where the time goes in v2:
time: 298 us
  Pallas kernels  278 us (93%)
  local copies, waits for them, and re-layouts  18.5 us (6%)
    pallas_call x1, Pallas kernels, first_part(): pl.pallas_call(first_kernel, out_shape=[shape((width, tokens), F32), shap...  158 us
    pallas_call x1, Pallas kernels, backward_part(): pl.pallas_call(backward_kernel, out_shape=[shape((16, 1, width), F32), sh...  120 us
    unnamed x17, local copies, waits for them, and re-layouts  11.5 us

profile of v2, /device:TPU:1, one launch (start us, length us, event | category | flops | bytes accessed | tf_op | source)
XLA Modules:
  0.0 297.5 jit_solution(1358477491056868013)
XLA Ops:
  0.6 1.3 broadcast_in_dim.17.upb_ref
  1.9 1.3 broadcast_in_dim.18.outb_ref
  3.2 1.3 broadcast_in_dim.19.downb_ref
  4.4 158.3 %shard_map.220 = (f32[768,512]{1,0:T(8,128)}, bf16[4,192,512]{2,1,0:T(8,128)(2,1)}, bf16[4,192,512]{2,1,0:T(8,128)(2,1)}, bf16[4,576,512]{2,1,0:T(8,128)(2,1)}, ...) custom-call(f32[192,2048]{1,0:T(8,128)} %stream_ref.3, ...), custom_call_target="tpu_custom_call" | custom-call | tf_op jit(solution)/shard_map/pallas_call | solution.py:1285
  162.7 120.1 %shard_map.221 = (f32[16,1,768]{2,1,0:T(1,128)}, f32[192,2048]{1,0:T(8,128)}, f32[192,2048]{1,0:T(8,128)}, f32[576,768]{1,0:T(8,128)}, f32[4,2,96,768]{3,2,1,0:T...) custom-call(bf16[4,192,512]{2,1,0:T(8,128)(2,1)} %get-tuple-element.38.gctx_ref, ...), custom_call_target="tpu_custom_call" | custom-call | tf_op jit(solution)/shard_map/pallas_call | solution.py:595
  282.8 1.3 slice_reduce_fusion
  284.2 0.6 constant_dynamic-slice_fusion
  284.8 0.7 constant_dynamic-slice_fusion.1
  285.5 0.6 slice.24
  286.1 0.0 copy-start.3
  286.1 2.8 copy.34
  288.9 0.0 copy-done.3
  288.9 0.0 copy-start.2
  288.9 1.1 copy.35
  290.1 0.9 copy-done.2
  291.0 0.0 copy-start.4
  291.0 0.0 copy-start.1
  291.0 1.2 copy.36
  292.2 0.2 copy-done.4
  292.4 0.8 copy.37
  293.2 0.4 copy-done.1
  293.6 1.4 copy.38
  295.0 1.1 copy-done
  296.1 1.4 copy.39
  (2 shorter events, 0.0 us)
Async XLA Ops:
  286.1 2.8 copy-start.3
  288.9 2.0 copy-start.2
  291.0 1.4 copy-start.4
  291.0 2.7 copy-start.1
  293.6 2.5 copy-start

commit v3 on v2

--- a/solution.py
+++ b/solution.py
@@ -351,6 +351,14 @@
     for copy in own[:-1]:
         copy.wait()
     copies = stage_two(grads[:2])
+    for k in range(GROUP):
+        swaps.append(
+            (
+                delta_ref.at[k], m_in.at[quarter], b_send.at[GROUP + k],
+                b_recv.at[GROUP + quarter], place, (row, k), do,
+            )
+        )
+        send_block(*swaps[GROUP + k])
     not_last = jnp.logical_or(
         mp < GROUP - 1, lax.broadcasted_iota(jnp.int32, (columns, 128), 0) < columns - 1
     )
@@ -368,14 +376,6 @@
 
     for k in range(GROUP):
         pltpu.make_async_copy(gctx_ref.at[k], gall.at[k], b_recv.at[k]).wait()
-    for k in range(GROUP):
-        swaps.append(
-            (
-                delta_ref.at[k], m_in.at[quarter], b_send.at[GROUP + k],
-                b_recv.at[GROUP + quarter], place, (row, k), do,
-            )
-        )
-        send_block(*swaps[GROUP + k])
     back_block(3)
     to_sibling(3)
     weight_terms(3)
@@ -412,6 +412,8 @@
     for side, (first, second) in enumerate(bits):
         for n, piece in enumerate((flip(do, first), flip(flip(do, first), second))):
             q_copies.append(post(gq.at[piece, :, sides[side]], q_one.at[side, n], column(first)))
+
+    copies = stage_four(copies)
 
     @pl.when(half == 0)
     def _():
@@ -472,7 +474,6 @@
     small_one = post(small_a, small_b.at[0], sibling)
 
     arrived(q_copies)
-    copies = stage_four(copies)
     q_copies = []
     for side, (first, second) in enumerate(bits):
         for n, piece in ((1, flip(do, second)), (0, do)):
@@ -668,7 +669,7 @@
 
 
 def first_kernel(
-    stream_ref, cot_ref, seg_ref, gain1_ref, gain2_ref, qv_ref, upb_ref, outb_ref, downb_ref,
+    stream_ref, cot_ref, seg_ref, gain1_ref, gain2_ref, qv_ref, bias_ref,
     qkvw_ref, up_own, down_own, out_own,
     mine_ref, heads_ref, rest_ref, qkv_ref, lse_ref, normed_ref, smalls_ref, headw_ref, segs_ref,
     stat_ref, delta_ref, gctx_ref, gnorm_ref, sums_ref, mine_up, one_up, mine_down, one_down, dout_ref,
@@ -712,7 +713,7 @@
     smalls_ref[mp, 0:1, :columns] = gain1_ref[...]
     smalls_ref[mp, 1:2, :columns] = gain2_ref[...]
     smalls_ref[mp, 2:4, :columns] = qv_ref[...]
-    smalls_ref[mp, 4:5] = upb_ref[...]
+    smalls_ref[mp, 4:5] = bias_ref[0:1]
     greet(neighbours(do, di, mp))
     is_last = jnp.logical_and(
         mp == GROUP - 1, lax.broadcasted_iota(jnp.int32, (columns, tokens), 0) == columns - 1
@@ -1045,7 +1046,7 @@
                     )
                 )
     start(out_loads)
-    out_bias = jnp.broadcast_to(outb_ref[...], (8, width)).T[:, 0:1]
+    out_bias = bias_ref[...].T[:, 1:2]
     def cotangent_at(at):
         return grad_ref[:, :, at].reshape(width, 128).astype(F32)
 
@@ -1197,7 +1198,7 @@
     combine(GROUP - 1, (GROUP - 1) % 2)
     for args in x_args:
         sent_block(*args)
-    mlp_y = mlp[...] + downb_ref[...]
+    mlp_y = mlp[...] + bias_ref[2:3]
     pre[...] = mlp_y - jnp.sum(mlp_y, axis=1, keepdims=True) / width
 
     def mixed_delta(at):
@@ -1303,7 +1304,7 @@
         + [shape(half, BF), shape((2,) + half[1:], BF)] * 2
         + [shape((GROUP, 2, GROUP) + out_rows, BF)]
         + [shape((GROUP, 2, GROUP) + p, BF) for p in (rows, rows, out_rows)],
-        in_specs=[anywhere] * 2 + [vmem] * 7 + [anywhere] * 4,
+        in_specs=[anywhere] * 2 + [vmem] * 5 + [anywhere] * 4,
         out_specs=[vmem] * 19 + [anywhere] * 3,
         scratch_shapes=[
             bf(*slabs), bf(*slabs), bf(heads, GROUP, tokens, HD),
@@ -1334,9 +1335,11 @@
 ):
     columns = stream.shape[0]
     mp = lax.axis_index("mp")
-    smalls_in = [
-        ln1_gain[None], ln2_gain[None], qv_bias, up_bias[None], out_bias[None], down_bias[None]
-    ]
+    kind = lax.broadcasted_iota(jnp.int32, (8, up_bias.shape[0]), 0)
+    biases = jnp.where(
+        kind == 0, up_bias[None], jnp.where(kind == 1, out_bias[None], down_bias[None])
+    )
+    smalls_in = [ln1_gain[None], ln2_gain[None], qv_bias, biases]
     (
         mine, heads_out, heads_rest, qkv, lse, normed_one, smalls, head_weight, segs, stat,
         delta, grad_context, grad_norm_two, sums, *rest,

time: 298 us -> 289 us (0.970)
  Pallas kernels: 278 us -> 272 us
  local copies, waits for them, and re-layouts: 18.5 us -> 15.3 us
    pallas_call x1, Pallas kernels: 120 us -> 113 us  [backward_part(): pl.pallas_call(backward_kernel, out_shape=[shape((16, 1, width), F32), sh...]
    broadcast_in_dim x3 -> x0, local copies, waits for them, and re-layouts: 3.8 us -> none  [the longest x1 1.27 us: local(): up_bias[None]]
where the time goes in v3:
time: 289 us
  Pallas kernels  272 us (94%)
  local copies, waits for them, and re-layouts  15.3 us (5%)
    pallas_call x1, Pallas kernels, first_part(): pl.pallas_call(first_kernel, out_shape=[shape((width, tokens), F32), shap...  158 us
    pallas_call x1, Pallas kernels, backward_part(): pl.pallas_call(backward_kernel, out_shape=[shape((16, 1, width), F32), sh...  113 us
    unnamed x17, local copies, waits for them, and re-layouts  11.5 us

profile of v3, /device:TPU:1, one launch (start us, length us, event | category | flops | bytes accessed | tf_op | source)
XLA Modules:
  0.0 289.0 jit_solution(16811770244649511247)
XLA Ops:
  0.7 1.4 select_select_fusion.bias_ref
  2.1 158.2 %shard_map.220 = (f32[768,512]{1,0:T(8,128)}, bf16[4,192,512]{2,1,0:T(8,128)(2,1)}, bf16[4,192,512]{2,1,0:T(8,128)(2,1)}, bf16[4,576,512]{2,1,0:T(8,128)(2,1)}, ...) custom-call(f32[192,2048]{1,0:T(8,128)} %stream_ref.3, ...), custom_call_target="tpu_custom_call" | custom-call | tf_op jit(solution)/shard_map/pallas_call | solution.py:1286
  160.3 113.4 %shard_map.221 = (f32[16,1,768]{2,1,0:T(1,128)}, f32[192,2048]{1,0:T(8,128)}, f32[192,2048]{1,0:T(8,128)}, f32[576,768]{1,0:T(8,128)}, f32[4,2,96,768]{3,2,1,0:T...) custom-call(bf16[4,192,512]{2,1,0:T(8,128)(2,1)} %get-tuple-element.38.gctx_ref, ...), custom_call_target="tpu_custom_call" | custom-call | tf_op jit(solution)/shard_map/pallas_call | solution.py:596
  273.7 1.3 slice_reduce_fusion
  275.0 0.6 constant_dynamic-slice_fusion.2
  275.7 0.6 constant_dynamic-slice_fusion
  276.3 0.7 constant_dynamic-slice_fusion.1
  277.0 0.6 slice.24
  277.6 0.0 copy-start.3
  277.6 2.8 copy.34
  280.4 0.0 copy-done.3
  280.4 0.0 copy-start.2
  280.4 1.1 copy.35
  281.6 0.9 copy-done.2
  282.5 0.0 copy-start.4
  282.5 0.0 copy-start.1
  282.5 1.2 copy.36
  283.7 0.2 copy-done.4
  283.9 0.8 copy.37
  284.7 0.4 copy-done.1
  285.1 0.0 copy-start
  285.1 1.4 copy.38
  286.5 1.1 copy-done
  287.6 1.4 copy.39
  (2 shorter events, 0.0 us)
Async XLA Ops:
  277.6 2.8 copy-start.3
  280.4 2.0 copy-start.2
  282.5 1.4 copy-start.4
  282.5 2.7 copy-start.1
  285.1 2.5 copy-start

commit v4 on v3

--- a/solution.py
+++ b/solution.py
@@ -392,12 +392,6 @@
     across_row(2)
     weight_terms(1)
     copies += stage_three(out_copies, grads[2:])
-    for k in range(GROUP):
-        pltpu.make_async_copy(delta_ref.at[k], m_in.at[k], b_recv.at[GROUP + k]).wait()
-    mixed_load.wait()
-    add_local(m_in)
-    mixed_out = pltpu.make_async_copy(local_in, mixed_ref, own_sem.at[10])
-    mixed_out.start()
     back_block(0)
     to_sibling(0)
     across_row(1)
@@ -414,6 +408,13 @@
             q_copies.append(post(gq.at[piece, :, sides[side]], q_one.at[side, n], column(first)))
 
     copies = stage_four(copies)
+
+    for k in range(GROUP):
+        pltpu.make_async_copy(delta_ref.at[k], m_in.at[k], b_recv.at[GROUP + k]).wait()
+    mixed_load.wait()
+    add_local(m_in)
+    mixed_out = pltpu.make_async_copy(local_in, mixed_ref, own_sem.at[10])
+    mixed_out.start()
 
     @pl.when(half == 0)
     def _():

time: 289 us -> 289 us (level)
  no operation moved by 1% of the time
where the time goes in v4:
time: 289 us
  Pallas kernels  271 us (94%)
  local copies, waits for them, and re-layouts  15.3 us (5%)
    pallas_call x1, Pallas kernels, first_part(): pl.pallas_call(first_kernel, out_shape=[shape((width, tokens), F32), shap...  158 us
    pallas_call x1, Pallas kernels, backward_part(): pl.pallas_call(backward_kernel, out_shape=[shape((16, 1, width), F32), sh...  113 us
    unnamed x17, local copies, waits for them, and re-layouts  11.5 us

profile of v4, /device:TPU:1, one launch (start us, length us, event | category | flops | bytes accessed | tf_op | source)
XLA Modules:
  0.0 288.7 jit_solution(17391364025050941139)
XLA Ops:
  0.7 1.4 select_select_fusion.bias_ref
  2.1 158.2 %shard_map.220 = (f32[768,512]{1,0:T(8,128)}, bf16[4,192,512]{2,1,0:T(8,128)(2,1)}, bf16[4,192,512]{2,1,0:T(8,128)(2,1)}, bf16[4,576,512]{2,1,0:T(8,128)(2,1)}, ...) custom-call(f32[192,2048]{1,0:T(8,128)} %stream_ref.3, ...), custom_call_target="tpu_custom_call" | custom-call | tf_op jit(solution)/shard_map/pallas_call | solution.py:1287
  160.3 113.1 %shard_map.221 = (f32[16,1,768]{2,1,0:T(1,128)}, f32[192,2048]{1,0:T(8,128)}, f32[192,2048]{1,0:T(8,128)}, f32[576,768]{1,0:T(8,128)}, f32[4,2,96,768]{3,2,1,0:T...) custom-call(bf16[4,192,512]{2,1,0:T(8,128)(2,1)} %get-tuple-element.38.gctx_ref, ...), custom_call_target="tpu_custom_call" | custom-call | tf_op jit(solution)/shard_map/pallas_call | solution.py:597
  273.4 1.3 slice_reduce_fusion
  274.7 0.6 constant_dynamic-slice_fusion.2
  275.4 0.6 constant_dynamic-slice_fusion
  276.0 0.7 constant_dynamic-slice_fusion.1
  276.7 0.6 slice.24
  277.3 0.0 copy-start.3
  277.3 2.8 copy.34
  280.1 0.0 copy-done.3
  280.1 0.0 copy-start.2
  280.1 1.1 copy.35
  281.2 0.9 copy-done.2
  282.1 0.0 copy-start.4
  282.1 0.0 copy-start.1
  282.1 1.2 copy.36
  283.4 0.2 copy-done.4
  283.6 0.8 copy.37
  284.4 0.4 copy-done.1
  284.8 0.0 copy-start
  284.8 1.4 copy.38
  286.2 1.1 copy-done
  287.3 1.4 copy.39
  (2 shorter events, 0.0 us)
Async XLA Ops:
  277.3 2.8 copy-start.3
  280.1 2.0 copy-start.2
  282.1 1.4 copy-start.4
  282.1 2.7 copy-start.1
  284.8 2.5 copy-start
